TPU v7x, 512 devices: a whole 4x8x8 slice. The times are simulated.
512 devices in a mesh: tm: 64 (over y, x, core), src: 8 (over z).
Axes of the slice: x: 4, y: 8, z: 8, core: 2. Of those that a mesh axis runs over, the one named last changes fastest.
Arguments:
- src_partials: float32 [5, 786432], P(None, ('tm', 'src')), may hold values from -3 to 3
- att_geom: float32 [4, 786432], P(None, ('tm', 'src')), may hold values from -2.5 to 2.5
- spline_frac: float32 [786432], P(('tm', 'src')), may hold values from 0 to 1
- cal_partials: float32 [6, 786432], P(None, ('tm', 'src')), may hold values from -2 to 2
- residual: float32 [786432], P(('tm', 'src')), may hold values from -6 to 6
- weight: float32 [786432], P(('tm', 'src')), may hold values from 0.1 to 1
- source_ids: int32 [786432], P(('tm', 'src')), may hold values from 0 to 1023, as said below
- knot_ids: int32 [786432], P(('tm', 'src')), may hold values from 0 to 16380, as said below
- ccd_ids: int32 [786432], P(('tm', 'src')), may hold values from 0 to 255
Outputs:
- src_normal: float32 [5, 5, 524288], P(None, None, ('tm', 'src'))
- src_rhs: float32 [5, 524288], P(None, ('tm', 'src'))
- att_normal: float32 [4, 4, 4, 16384], P(None, None, None, 'tm')
- att_rhs: float32 [4, 16384], P(None, 'tm')
- cal_normal: float32 [6, 6, 16384], P(None, None, 'tm')
- cal_rhs: float32 [6, 16384], P(None, 'tm')
Inputs may be any that keep to these rules, and one draw needn't show every extreme that they name: `source_ids`: within each block of 1536 observations (blocks in the order of the tm+src placement) the source numbers do not decrease. `knot_ids`: among the rows of one device, at most 48 fall in any one time segment (knot index // 256); within every source shard some time segment holds exactly 48 rows of every device of that shard.
All inputs are finite; a program needn't handle non-finite values.
Results may differ from a plain program's by a relative error of at most 0.00016.
Values sent between devices are 32-bit elements; how exact they have to be, the bound alone decides.
No kernel may reach another device: no remote copies, remote signals or barrier semaphores. Data moves between devices by JAX's collectives and lax.ppermute only.
A program may use at most 64 MiB of HBM per device.

v0:
```python
import math

import jax
import jax.numpy as jnp
from jax import lax
from jax.sharding import PartitionSpec as P

SRC_DEV = 1024
KNOT_DEV = 256
CAL_DEV = 256


PRECISE = lax.Precision.HIGHEST


def passed_along(block, axis, distance):
    devices = range(lax.axis_size(axis))
    route = [(i - distance, i) for i in devices if i - distance in devices]
    return lax.ppermute(block, axis, route)


def spline_basis(frac):
    remain = 1.0 - frac
    square = frac * frac
    cubic_term = square * frac
    return jnp.stack(
        [
            remain * remain * remain / 6.0,
            (3.0 * cubic_term - 6.0 * square + 4.0) / 6.0,
            (-3.0 * cubic_term + 3.0 * square + 3.0 * frac + 1.0) / 6.0,
            cubic_term / 6.0,
        ]
    )


def spline_rows(frac, geom):
    return spline_basis(frac)[:, None, :] * geom[None, :, :]


def row_terms(partials, cal_rows, weight_row, resid_row):
    weighted = weight_row * resid_row
    width = weight_row.shape[0]
    pieces = []
    for band_gap in range(4):
        for first_knot in range(4 - band_gap):
            pieces.append(
                (
                    partials[first_knot][:, None, :]
                    * partials[first_knot + band_gap][None, :, :]
                    * weight_row
                ).reshape(-1, width)
            )
    for first_knot in range(4):
        pieces.append(partials[first_knot] * weighted)
    cal_terms = jnp.concatenate(
        [
            (cal_rows[:, None, :] * cal_rows[None, :, :] * weight_row).reshape(-1, width),
            cal_rows * weighted,
        ],
        0,
    )
    return (jnp.concatenate(pieces, 0), cal_terms)


def local(
    src_partials,
    att_geom,
    spline_frac,
    cal_partials,
    residual,
    weight,
    source_ids,
    knot_ids,
    ccd_ids,
):
    obs_count = residual.shape[0]
    src_count = src_partials.shape[0]
    comp_count = att_geom.shape[0]
    cal_count = cal_partials.shape[0]
    att_span = 4 * comp_count
    weighted = weight * residual
    outer_terms = (src_partials[:, None, :] * src_partials[None, :, :] * weight).reshape(
        src_count * src_count, obs_count
    )
    stacked = jnp.concatenate([outer_terms, src_partials * weighted], 0)
    src_columns = lax.iota(jnp.int32, SRC_DEV)
    src_step = math.gcd(128, obs_count)

    def add_sources(block_turn, totals):
        begin_col = block_turn * src_step
        term_block = lax.dynamic_slice_in_dim(stacked, begin_col, src_step, 1)
        id_block = lax.dynamic_slice_in_dim(source_ids, begin_col, src_step, 0)
        onehot = (id_block[:, None] == src_columns[None, :]).astype(jnp.float32)
        return totals + jnp.dot(
            term_block, onehot, precision=PRECISE, preferred_element_type=jnp.float32
        )

    src_sums = lax.fori_loop(
        0, obs_count // src_step, add_sources, jnp.zeros((stacked.shape[0], SRC_DEV), jnp.float32)
    )
    tm_count = lax.axis_size("tm")
    capacity = 2 * obs_count // tm_count
    segment = knot_ids // KNOT_DEV
    seg_columns = lax.iota(jnp.int32, tm_count)
    counts = jnp.sum((segment[:, None] == seg_columns[None, :]).astype(jnp.int32), 0)
    starts = jnp.cumsum(counts) - counts
    by_segment = jnp.argsort(segment, stable=True)
    sorted_seg = segment[by_segment]
    sorted_start = jnp.sum(
        (sorted_seg[:, None] == seg_columns[None, :]).astype(jnp.int32) * starts[None, :], 1
    )
    slot_sorted = sorted_seg * capacity + lax.iota(jnp.int32, obs_count) - sorted_start
    slot_index = jnp.zeros((obs_count,), jnp.int32).at[by_segment].set(slot_sorted)
    payload = jnp.concatenate(
        [
            spline_rows(spline_frac, att_geom).reshape(att_span, obs_count),
            cal_partials,
            weight[None, :],
            residual[None, :],
        ],
        0,
    )
    labels = jnp.stack([knot_ids - segment * KNOT_DEV, ccd_ids], 0)
    send_rows = (
        jnp.zeros((payload.shape[0], tm_count * capacity), jnp.float32)
        .at[:, slot_index]
        .set(payload)
    )
    send_labels = jnp.zeros((2, tm_count * capacity), jnp.int32).at[:, slot_index].set(labels)
    got_rows, got_labels = (
        lax.all_to_all(send_rows, "tm", split_axis=1, concat_axis=1, tiled=True),
        lax.all_to_all(send_labels, "tm", split_axis=1, concat_axis=1, tiled=True),
    )

    def unpack(row_block):
        partials = row_block[:att_span].reshape(4, comp_count, -1)
        others = row_block[att_span:]
        return (partials, others[:cal_count], others[cal_count], others[cal_count + 1])

    total_rows = tm_count * capacity
    time_step = math.gcd(512, total_rows)
    knot_columns = lax.iota(jnp.int32, KNOT_DEV)
    ccd_columns = lax.iota(jnp.int32, CAL_DEV)
    att_terms_count = 10 * comp_count * comp_count + 4 * comp_count
    cal_terms_count = cal_count * cal_count + cal_count

    def add_times(block_turn, totals):
        begin_col = block_turn * time_step
        row_block = lax.dynamic_slice_in_dim(got_rows, begin_col, time_step, 1)
        label_block = lax.dynamic_slice_in_dim(got_labels, begin_col, time_step, 1)
        partials, cal_rows, weight_row, resid_row = unpack(row_block)
        att_terms, cal_terms = row_terms(partials, cal_rows, weight_row, resid_row)
        knot_hot = (label_block[0][:, None] == knot_columns[None, :]).astype(jnp.float32)
        ccd_hot = (label_block[1][:, None] == ccd_columns[None, :]).astype(jnp.float32)
        return (
            totals[0]
            + jnp.dot(att_terms, knot_hot, precision=PRECISE, preferred_element_type=jnp.float32),
            totals[1]
            + jnp.dot(cal_terms, ccd_hot, precision=PRECISE, preferred_element_type=jnp.float32),
        )

    att_sums, cal_sums = lax.fori_loop(
        0,
        total_rows // time_step,
        add_times,
        (
            jnp.zeros((att_terms_count, KNOT_DEV), jnp.float32),
            jnp.zeros((cal_terms_count, CAL_DEV), jnp.float32),
        ),
    )
    pair_size = comp_count * comp_count
    offset_row = 0
    band_parts = []
    for band_gap in range(4):
        banded = jnp.zeros((pair_size, KNOT_DEV + 3), jnp.float32)
        for first_knot in range(4 - band_gap):
            banded = banded.at[:, first_knot : first_knot + KNOT_DEV].add(
                att_sums[offset_row : offset_row + pair_size]
            )
            offset_row = offset_row + pair_size
        band_parts.append(banded)
    banded = jnp.zeros((comp_count, KNOT_DEV + 3), jnp.float32)
    for first_knot in range(4):
        banded = banded.at[:, first_knot : first_knot + KNOT_DEV].add(
            att_sums[offset_row : offset_row + comp_count]
        )
        offset_row = offset_row + comp_count
    band_parts.append(banded)
    extended = jnp.concatenate(band_parts, 0)
    summed, cal_total = lax.psum((extended, cal_sums), "src")
    received = passed_along(summed[:, KNOT_DEV:], "tm", 1)
    attitude = summed[:, :KNOT_DEV].at[:, :3].add(received)
    src_normal = src_sums[: src_count * src_count].reshape(src_count, src_count, SRC_DEV)
    src_rhs = src_sums[src_count * src_count :]
    att_normal = attitude[: 4 * pair_size].reshape(4, comp_count, comp_count, KNOT_DEV)
    att_rhs = attitude[4 * pair_size :]
    cal_normal = cal_total[: cal_count * cal_count].reshape(cal_count, cal_count, CAL_DEV)
    cal_rhs = cal_total[cal_count * cal_count :]
    return (src_normal, src_rhs, att_normal, att_rhs, cal_normal, cal_rhs)


def solution(mesh):
    in_specs = (
        P(None, ("tm", "src")),
        P(None, ("tm", "src")),
        P(("tm", "src")),
        P(None, ("tm", "src")),
        P(("tm", "src")),
        P(("tm", "src")),
        P(("tm", "src")),
        P(("tm", "src")),
        P(("tm", "src")),
    )
    out_specs = (
        P(None, None, ("tm", "src")),
        P(None, ("tm", "src")),
        P(None, None, None, "tm"),
        P(None, "tm"),
        P(None, None, "tm"),
        P(None, "tm"),
    )
    return jax.shard_map(local, mesh=mesh, in_specs=in_specs, out_specs=out_specs, check_vma=False)
```

profile of v0, /device:TPU:6, one launch (start us, length us, event | category | flops | bytes accessed | tf_op | source)
XLA Modules:
  0.0 223.5 jit_solution(1008417814387115134)
XLA Ops:
  7.2 0.7 multiply_subtract_fusion
  8.3 5.0 %sort.17 = (s32[1536]{0:T(1024)}, s32[1536]{0:T(1024)S(1)}) sort(s32[1536]{0:T(1024)S(1)} %get-tuple-element.539, s32[1536]{0:T(1024)S(1)} %iota.39), dimensions={0}, to_apply=%region_3.4 | sort | flops 16896 | bytes 24576 | tf_op jit(solution)/shard_map/jit(argsort)/sort | solution.py:107
  13.4 8.4 %gather_fusion = s32[1536]{0:T(1024)S(1)} fusion(s32[1536]{0:T(1024)S(1)} %get-tuple-element.539, s32[2048]{0:T(1024)S(1)} %pad_clamp_fusion), kind=kCustom, calls=%fused_computation | custom fusion | bytes 18432 | tf_op jit(solution)/shard_map/gather | solution.py:108
  21.9 6.2 %scatter_custom_fusion = s32[1536]{0:T(1024)S(1)} fusion(s32[1536]{0:T(1024)S(1)} %compare_select_fusion.1, s32[1536]{0:T(1024)S(1)} %add_subtract_fusion, s32[]{:T(128)} %constant.416.clone.1), kind=kCustom, calls=%fused_computation.112 | custom fusion | bytes 6148 | tf_op jit(solution)/shard_map/scatter | solution.py:113
  28.6 4.7 %scatter_custom_fusion.2 = s32[2,3072]{0,1:T(8,128)S(1)} fusion(s32[1536]{0:T(1024)S(1)} %compare_select_fusion, s32[1536,2]{1,0:T(8,128)S(1)} %copy.36, s32[]{:T(128)} %constant.416.clone.1), kind=kCustom, calls=%fused_computation.51 | custom fusion | bytes 24580 | tf_op jit(solution)/shard_map/scatter | solution.py:129
  33.3 1.2 copy.37
  34.5 10.6 %all-to-all-start.1 = ((s32[2,64,48]{2,0,1:T(2,128)}), s32[2,64,48]{2,0,1:T(2,128)S(1)}, u32[]{:S(2)}, u32[]{:S(2)}) async-start(s32[2,64,48]{2,0,1:T(2,128)} %copy.37), calls=%async_computation.1 | async-start | bytes 131072 | tf_op jit(solution)/shard_map/all_to_all | solution.py:132
  45.8 4.7 %scatter_custom_fusion.1 = f32[24,3072]{0,1:T(8,128)S(1)} fusion(s32[1536]{0:T(1024)S(1)} %compare_select_fusion, f32[1536,24]{1,0:T(8,128)S(1)} %copy.33, f32[]{:T(128)} %constant.417.clone.1), kind=kCustom, calls=%fused_computation.53 | custom fusion | bytes 294916 | tf_op jit(solution)/shard_map/scatter | solution.py:127
  50.6 0.4 copy.34
  51.0 1.5 reshape.615
  52.5 0.6 compare_reduce_fusion.3
  53.1 0.6 compare_reduce_fusion.2
  53.8 0.6 compare_reduce_fusion.1
  54.4 10.3 %all-to-all-start = ((f32[64,1,1152]{2,1,0:T(1,128)}), f32[64,1,1152]{2,1,0:T(1,128)S(1)}, u32[]{:S(2)}, u32[]{:S(2)}) async-start(f32[64,1,1152]{2,1,0:T(1,128)} %reshape.615), calls=%async_computation | async-start | bytes 589824 | tf_op jit(solution)/shard_map/all_to_all | solution.py:131
  65.1 12.3 %all-to-all-done = f32[64,1,1152]{2,1,0:T(1,128)S(1)} async-done(((f32[64,1,1152]{2,1,0:T(1,128)}), f32[64,1,1152]{2,1,0:T(1,128)S(1)}, u32[]{:S(2)}, u32[]{:S(2)}) %all-to-all-start) | async-done | bytes 294944 | tf_op jit(solution)/shard_map/all_to_all | solution.py:131
  77.3 0.5 broadcast.484
  77.8 1.3 reduce.55
  79.7 0.4 all_to_all.18
  80.1 9.6 %while.48 = (s32[]{:T(128)}, f32[176,256]{1,0:T(8,128)S(1)}, f32[42,256]{1,0:T(8,128)S(1)}, f32[24,3072]{1,0:T(8,128)S(1)}, s32[2,3072]{1,0:T(2,128)S(1)}, /*ind...) while((s32[]{:T(128)}, f32[176,256]{1,0:T(8,128)S(1)}, ...), condition=%wide.region_11.12_spmd.clone.clone, body=%wide.region_10.11_spmd.clone.clone.sunk | while | flops 343492096 | bytes 3830094 | solution.py:162
  80.8 0.5 convolution_add_fusion.7
  82.4 0.5 convolution_add_fusion.7
  84.0 0.5 convolution_add_fusion.7
  85.6 0.5 convolution_add_fusion.7
  87.2 0.5 convolution_add_fusion.7
  88.8 0.5 convolution_add_fusion.7
  89.8 0.7 slice_select_fusion.4
  90.4 0.7 slice_select_fusion.3
  91.1 0.7 add_select_fusion.8
  91.8 1.4 slice_select_fusion.2
  93.5 0.6 add_select_fusion.7
  94.8 1.9 slice_select_fusion.1
  97.1 0.4 scatter-add.59
  97.5 1.9 slice_select_fusion
  99.5 0.4 scatter-add.60
  100.2 0.4 scatter-add.55
  100.6 0.4 scatter-add.64
  101.1 0.6 copy-done.1
  101.8 13.8 %while.47 = (s32[]{:T(128)}, f32[30,1024]{1,0:T(8,128)S(1)}, f32[30,1536]{1,0:T(8,128)S(1)}, s32[1536]{0:T(1024)}, s32[]{:T(128)}, /*index=5*/s32[]{:T(128)}, s32[]{:T(128)}, s32[]{:T(128)}) while((s32[]{:T(128)}, f32[30,1024]{1,0:T(8,128)S(1)}, f32[30,1536]{1,0:T(8,128)S(1)}, s32[1536]{0:T(1024)}, s32[]{:T(128)}, ...), condition=%wide.region_1.0_spmd.clone, body=%wide.region_0.0_spmd.clone.sunk | while | flops 47378440 | bytes 272021 | solution.py:98
  101.8 0.8 dynamic_slice.41
  102.9 0.8 dynamic_slice.41
  104.1 0.8 dynamic_slice.41
  105.2 0.8 dynamic_slice.41
  106.4 0.8 dynamic_slice.41
  107.5 0.8 dynamic_slice.41
  108.7 0.8 dynamic_slice.41
  109.8 0.8 dynamic_slice.41
  111.0 0.8 dynamic_slice.41
  112.1 0.8 dynamic_slice.41
  113.3 0.8 dynamic_slice.41
  114.4 0.8 dynamic_slice.41
  115.6 0.6 slice.445
  116.2 0.7 reshape.567
  116.9 0.6 compare_reduce_fusion
  117.5 62.4 %all-reduce.7.cloned.1.call-done = f32[68,259]{1,0:T(8,128)} async-done(((f32[68,259]{1,0:T(8,128)}), f32[68,259]{1,0:T(8,128)}) %all-reduce.7.cloned.1.call-update) | async-done | bytes 70464 | tf_op jit(solution)/shard_map/psum | solution.py:190
  180.0 0.8 slice.503
  180.7 1.9 collective-permute-start
  182.6 28.7 %psum.15 = f32[42,256]{1,0:T(8,128)S(1)} all-reduce(f32[42,256]{1,0:T(8,128)S(1)} %get-tuple-element.417), channel_id=1, replica_groups=mesh['tm'=64,'src'=8] {'src'}, use_global_device_ids=true, to_apply=%region_16.17 | all-reduce | flops 10752 | bytes 86016 | tf_op jit(solution)/shard_map/psum | solution.py:190
  211.4 0.6 slice.507
  212.0 0.6 reshape.571
  212.6 0.9 slice.501
  213.5 1.4 add_select_fusion
  214.9 0.4 scatter-add.74
  215.4 0.6 slice.505
  216.0 0.6 reshape.570
  (214 shorter events, 14.2 us)
Async XLA Ops:
  13.4 14.8 %copy-start.7 = (s32[1536]{0:T(1024)S(1)}, s32[1536]{0:T(1024)}, u32[]{:S(2)}) copy-start(s32[1536]{0:T(1024)} %param.51) | copy-start | bytes 18436
  28.5 16.6 %copy-start.6 = (f32[1536]{0:T(1024)S(1)}, f32[1536]{0:T(1024)}, u32[]{:S(2)}) copy-start(f32[1536]{0:T(1024)} %param.45) | copy-start | bytes 18436
  28.5 16.7 %copy-start.5 = (f32[4,1536]{1,0:T(4,128)S(1)}, f32[4,1536]{1,0:T(4,128)}, u32[]{:S(2)}) copy-start(f32[4,1536]{1,0:T(4,128)} %param.44) | copy-start | bytes 73732
  28.5 16.8 %copy-start.2 = (f32[1536]{0:T(1024)S(1)}, f32[1536]{0:T(1024)}, u32[]{:S(2)}) copy-start(f32[1536]{0:T(1024)} %param.48) | copy-start | bytes 18436
  28.5 16.8 %copy-start.4 = (f32[1536]{0:T(1024)S(1)}, f32[1536]{0:T(1024)}, u32[]{:S(2)}) copy-start(f32[1536]{0:T(1024)} %param.47) | copy-start | bytes 18436
  28.6 16.8 %copy-start = (f32[5,1536]{1,0:T(8,128)S(1)}, f32[5,1536]{1,0:T(8,128)}, u32[]{:S(2)}) copy-start(f32[5,1536]{1,0:T(8,128)} %param.43) | copy-start | bytes 92164
  33.3 12.2 %copy-start.3 = (f32[6,1536]{1,0:T(8,128)S(1)}, f32[6,1536]{1,0:T(8,128)}, u32[]{:S(2)}) copy-start(f32[6,1536]{1,0:T(8,128)} %param.46) | copy-start | bytes 110596
  34.5 19.9 %all-to-all-start.1 = ((s32[2,64,48]{2,0,1:T(2,128)}), s32[2,64,48]{2,0,1:T(2,128)S(1)}, u32[]{:S(2)}, u32[]{:S(2)}) async-start(s32[2,64,48]{2,0,1:T(2,128)} %copy.37), calls=%async_computation.1 | async-start | bytes 131072 | tf_op jit(solution)/shard_map/all_to_all | solution.py:132
  54.4 23.0 %all-to-all-start = ((f32[64,1,1152]{2,1,0:T(1,128)}), f32[64,1,1152]{2,1,0:T(1,128)S(1)}, u32[]{:S(2)}, u32[]{:S(2)}) async-start(f32[64,1,1152]{2,1,0:T(1,128)} %reshape.615), calls=%async_computation | async-start | bytes 589824 | tf_op jit(solution)/shard_map/all_to_all | solution.py:131
  64.7 115.3 %all-reduce.7.cloned.1.call-start = ((), (), s32[]{:S(2)}) async-start(), calls=%async_computation.2 | async-start | bytes 221184 | tf_op jit(solution)/shard_map/psum | solution.py:190
  101.1 0.6 copy-start.1
  180.7 32.8 %collective-permute-start = (f32[68,3]{1,0:T(8,128)S(1)}, f32[68,3]{1,0:T(8,128)S(1)}, u32[]{:S(2)}, u32[]{:S(2)}) collective-permute-start(f32[68,3]{1,0:T(8,128)S(1)} %slice.503), channel_id=1, source_target_pairs={{0,8},{8,16},{16,24},{24,32},{32,40},{40,48},{48,56},{56,64},{64,7... | collective-permute-start | bytes 2456 | tf_op jit(solution)/shard_map/ppermute | solution.py:19
Sparse Core Ops, SparseCore 0:
  101.9 78.0 all-reduce.6
where the time goes:
time: 224 us; the launch traced here: 223 us
  waiting for transfers between devices  74.7 us (33%)
  local copies, waits for them, and re-layouts  50.4 us (22%)
  blocking collectives  28.7 us (13%)
  starting transfers between devices  23 us (10%)
  other arithmetic  21.4 us (10%)
  between operations  14.7 us (7%)
  matrix products  9.44 us (4%)
    psum x1, waiting for transfers between devices, local(): summed, cal_total = lax.psum((extended, cal_sums), 'src')  62.4 us
    psum x1, blocking collectives, local(): summed, cal_total = lax.psum((extended, cal_sums), 'src')  28.7 us
    all_to_all x1, waiting for transfers between devices, local(): lax.all_to_all(send_rows, 'tm', split_axis=1, concat_axis=1, tiled=True)  12.3 us
    another operation x14, other arithmetic  12 us
    all_to_all x1, starting transfers between devices, local(): lax.all_to_all(send_labels, 'tm', split_axis=1, concat_axis=1, tiled=True)  10.6 us
    all_to_all x1, starting transfers between devices, local(): lax.all_to_all(send_rows, 'tm', split_axis=1, concat_axis=1, tiled=True)  10.3 us
    dynamic_slice x12, local copies, waits for them, and re-layouts, add_sources(): id_block = lax.dynamic_slice_in_dim(source_ids, begin_col, src_step, 0)  9.17 us
    gather x1, local copies, waits for them, and re-layouts, local(): sorted_seg = segment[by_segment]  8.39 us
  transfers between devices with their start and end apart: 4, of which 2 were waited for; matrix products, arithmetic and copies ran while one was open for 12% of the time, Pallas kernels for 0%

commit v1 on v0

v1 whole, which is shorter than its diff:
```python
import jax
import jax.numpy as jnp
from jax import lax
from jax.experimental import pallas as pl
from jax.experimental.pallas import tpu as pltpu
from jax.sharding import PartitionSpec as P

SRC_DEV = 1024
SEG = 256
LANES = 128
F32 = jnp.float32
BF16 = jnp.bfloat16

FIELDS = 14
HALO_FIELDS = 7
ATT_PAIRS = [(c, e) for c in range(4) for e in range(c, 4)]
CAL_PAIRS = [(p, q) for p in range(6) for q in range(p, 6)]
SRC_PAIRS = [(p, q) for p in range(5) for q in range(p, 5)]
GROUP_ROWS = [48, 40, 24, 16]
GROUP_START = [0, 48, 88, 112]
VMEM_LIMIT = 56 * 1024 * 1024


def nt_dot(left, right):
    return lax.dot_general(
        left, right, (((1,), (1,)), ((), ())), preferred_element_type=F32
    )


def split(x):
    high = x.astype(BF16)
    return high, (x - high.astype(F32)).astype(BF16)


def onehot(rows, first, ids):
    place = lax.broadcasted_iota(jnp.int32, (rows, ids.shape[1]), 0) + first
    return jnp.where(place == ids, 1.0, 0.0).astype(BF16)


def pack_kernel(geom, frac, cal, resid, weight, knot, ccd, out, hot_s, val_s):
    obs = knot.shape[1]
    segs = out.shape[0]
    chunk = 256
    blocks = obs // chunk
    knots = knot[...]
    seg = knots // SEG
    member = onehot(segs, 0, seg)
    before = lax.broadcasted_iota(jnp.int32, (chunk, chunk), 0) < lax.broadcasted_iota(
        jnp.int32, (chunk, chunk), 1
    )
    before = jnp.where(before, 1.0, 0.0).astype(BF16)
    counter = jnp.concatenate([before, jnp.ones((chunk, LANES), BF16)], 1)
    carry = jnp.zeros((segs, LANES), F32)
    ranks = []
    for b in range(blocks):
        here = member[:, b * chunk : (b + 1) * chunk]
        counts = jnp.dot(here, counter, preferred_element_type=F32)
        for half in range(chunk // LANES):
            cols = slice(half * LANES, (half + 1) * LANES)
            ranks.append(
                jnp.sum(here[:, cols].astype(F32) * (counts[:, cols] + carry), 0, keepdims=True)
            )
        carry = carry + counts[:, chunk:]
    rank = jnp.concatenate(ranks, 1).astype(jnp.int32)
    high = rank // 8
    low = rank - 8 * high
    third = high // 3
    high3 = high - 3 * third

    scale = jnp.sqrt(weight[...])
    geoms = geom[...] * scale
    cals = cal[...] * scale
    fields = [geoms[c : c + 1] for c in range(4)]
    fields += [frac[...], resid[...] * scale, (knots - SEG * seg).astype(F32)]
    fields += [cals[p : p + 1] for p in range(6)]
    fields += [ccd[...].astype(F32)]
    fields = jnp.concatenate(fields, 0)
    rounded = fields.astype(BF16).astype(F32)
    parts = (rounded, fields - rounded)
    low_is = lax.broadcasted_iota(jnp.int32, (8, obs), 0) == low
    low_is3 = [low_is & (high3 == h) for h in range(3)]
    zero = jnp.zeros((8, obs), F32)

    def spread(row, mask):
        return jnp.where(mask, row, 0.0)

    for i, part in enumerate(parts):
        rows = [part[f : f + 1] for f in range(FIELDS)]
        main = [spread(r, low_is) for r in rows] + [zero, zero]
        extra = [spread(rows[f], low_is3[h]) for f in range(2, HALO_FIELDS) for h in range(3)]
        extra = extra + [zero]
        for j in range(0, 16, 2):
            at = i * LANES + 8 * j
            val_s[0, at : at + 16, :] = jnp.concatenate(main[j : j + 2], 0).astype(BF16)
            val_s[1, at : at + 16, :] = jnp.concatenate(extra[j : j + 2], 0).astype(BF16)
    code = seg * 8 + high
    for j in range(0, 8 * segs, 64):
        hot_s[j : j + 64, :] = onehot(64, j, code)
    main = nt_dot(hot_s[...], val_s[0])
    main = main[:, :LANES] + main[:, LANES:]
    extra = nt_dot(onehot(2 * segs, 0, jnp.where(seg == segs - 1, -1, seg + 1 + segs * third)), val_s[1])
    extra = extra[:, :LANES] + extra[:, LANES:]
    lane = lax.broadcasted_iota(jnp.int32, (8 * segs, LANES), 1)
    shifted = jnp.concatenate([jnp.zeros((8, LANES), F32), main[:-8]], 0)
    shifted = pltpu.roll(shifted, 8 * FIELDS, 1)
    tiles = jnp.where(lane < 8 * FIELDS, main, shifted)
    out[...] = tiles.reshape(segs, 8, LANES)
    out[:, 6, :] = extra[:segs]
    out[:, 7, :] = extra[segs:]


def source_kernel(partials, resid, weight, ids, normal, rhs, left_s):
    obs = ids.shape[1]
    count = partials.shape[0]
    part = partials[...]
    rows = [part[p : p + 1] for p in range(count)]
    scaled = part * weight[...]
    scaled_rows = [scaled[p : p + 1] for p in range(count)]
    terms = [scaled_rows[p] * rows[q] for p, q in SRC_PAIRS]
    terms += [scaled_rows[p] * resid[...] for p in range(count)]
    terms += [jnp.zeros((32 - len(terms), obs), F32)]
    high, low = split(jnp.concatenate(terms, 0))
    left_s[0:32, :] = high
    left_s[32:64, :] = low
    left = left_s[...]
    step = 256
    for j in range(0, SRC_DEV, step):
        sums = nt_dot(left, onehot(step, j, ids[...]))
        sums = sums[:32] + sums[32:]
        for t, (p, q) in enumerate(SRC_PAIRS):
            normal[p, q : q + 1, j : j + step] = sums[t : t + 1]
            if p != q:
                normal[q, p : p + 1, j : j + step] = sums[t : t + 1]
        rhs[:, j : j + step] = sums[len(SRC_PAIRS) : len(SRC_PAIRS) + count]


def att_terms(rows, keep):
    geoms = [jnp.where(keep, rows[c], 0.0) for c in range(4)]
    frac, resid = rows[4], rows[5]
    remain = 1.0 - frac
    square = frac * frac
    cubic = square * frac
    basis = [
        remain * remain * remain * (1.0 / 6.0),
        (3.0 * cubic - 6.0 * square + 4.0) * (1.0 / 6.0),
        (-3.0 * cubic + 3.0 * square + 3.0 * frac + 1.0) * (1.0 / 6.0),
        cubic * (1.0 / 6.0),
    ]
    pairs = [geoms[c] * geoms[e] for c, e in ATT_PAIRS]
    weighted = [geoms[c] * resid for c in range(4)]
    terms = []
    for a in range(4):
        place = GROUP_START[a]
        for c in range(4):
            terms.append((place + c, basis[a] * weighted[c]))
        place = place + 4
        for d in range(4 - a):
            both = basis[a] * basis[a + d]
            for q in range(10):
                terms.append((place + q, both * pairs[q]))
            place = place + 10
        end = GROUP_START[a] + GROUP_ROWS[a]
        for t in range(place, end):
            terms.append((t, jnp.zeros_like(frac)))
    return terms


def time_kernel(got, out, att_f, halo_f, cal_f, att_l, halo_l, cal_l, knot_hot, halo_hot, ccd_hot):
    lane = lax.broadcasted_iota(jnp.int32, (8, LANES), 1)
    sub = lane % 8
    keep = sub < 6
    chunks = got.shape[0] * 8 // LANES
    halo_hot[0 : LANES - 16, :] = jnp.zeros((LANES - 16, halo_hot.shape[1]), BF16)
    for c in range(chunks):
        block = got[c * 16 : (c + 1) * 16].reshape(LANES, LANES)
        turned = block.T
        rows = [turned[8 * f : 8 * f + 8] for f in range(16)]
        for t, value in att_terms(rows, keep):
            att_f[c, pl.ds(t, 8, stride=LANES), :] = value
        cals = [jnp.where(keep, rows[7 + p], 0.0) for p in range(6)]
        terms = [cals[p] * cals[q] for p, q in CAL_PAIRS]
        terms += [cals[p] * rows[5] for p in range(6)]
        terms += [jnp.zeros_like(lane, F32)] * (32 - len(terms))
        for t, value in enumerate(terms):
            cal_f[c, pl.ds(t, 8, stride=32), :] = value
        halo = [rows[14], rows[15]]
        for h in range(2, HALO_FIELDS):
            value = jnp.zeros((8, LANES), F32)
            for r in range(6):
                moved = pltpu.roll(rows[(h - 2) * 3 + r % 3], LANES - (6 + r // 3 - r), 1)
                value = jnp.where(sub == r, moved, value)
            halo.append(value)
        for t, value in att_terms(halo, keep):
            halo_f[c, pl.ds(t, 8, stride=LANES), :] = value
        for l in range(8):
            cols = slice((c * 8 + l) * LANES, (c * 8 + l + 1) * LANES)
            att_l[0:LANES, cols], att_l[LANES:, cols] = split(att_f[c, l * LANES : (l + 1) * LANES, :])
            halo_l[0:LANES, cols], halo_l[LANES:, cols] = split(
                halo_f[c, l * LANES : (l + 1) * LANES, :]
            )
            cal_l[0:32, cols], cal_l[32:, cols] = split(cal_f[c, l * 32 : (l + 1) * 32, :])
            knot_hot[:, cols] = onehot(SEG, 0, rows[6][l : l + 1].astype(jnp.int32))
            ccd_hot[:, cols] = onehot(SEG, 0, rows[13][l : l + 1].astype(jnp.int32))
            halo_hot[LANES - 16 :, cols] = onehot(16, SEG - 16, halo[6][l : l + 1].astype(jnp.int32))
    main = nt_dot(att_l[...], knot_hot[...])
    edge = nt_dot(halo_l[...], halo_hot[...])
    sums = jnp.concatenate([edge[:LANES] + edge[LANES:], main[:LANES] + main[LANES:]], 1)
    total = sums[: GROUP_ROWS[0], LANES:]
    for a in range(1, 4):
        n = GROUP_ROWS[a]
        group = sums[GROUP_START[a] : GROUP_START[a] + n]
        group = pltpu.roll(group, a, 1)[:, LANES:]
        if n < GROUP_ROWS[0]:
            group = jnp.concatenate([group, jnp.zeros((GROUP_ROWS[0] - n, SEG), F32)], 0)
        total = total + group
    cal = nt_dot(cal_l[...], ccd_hot[...])
    cal = cal[:32] + cal[32:]
    for z in range(out.shape[0]):
        out[z, 0:48, :] = total
        out[z, 48:72, :] = cal[0:24]
        out[z, 44:47, :] = cal[24:27]


def final_kernel(parts, att_normal, att_rhs, cal_normal, cal_rhs, sum_s):
    total = parts[0]
    for z in range(1, parts.shape[0]):
        total = total + parts[z]
    sum_s[...] = total
    att_rhs[...] = sum_s[0:4, :]
    for d in range(4):
        for q, (c, e) in enumerate(ATT_PAIRS):
            row = sum_s[4 + 10 * d + q : 5 + 10 * d + q, :]
            att_normal[d, c, e : e + 1, :] = row
            if c != e:
                att_normal[d, e, c : c + 1, :] = row

    def cal_row(t):
        at = 48 + t if t < 24 else 20 + t
        return sum_s[at : at + 1, :]

    for t, (p, q) in enumerate(CAL_PAIRS):
        cal_normal[p, q : q + 1, :] = cal_row(t)
        if p != q:
            cal_normal[q, p : p + 1, :] = cal_row(t)
    for p in range(6):
        cal_rhs[p : p + 1, :] = cal_row(21 + p)


def call(kernel, out_shape, scratch, cost, *args):
    return pl.pallas_call(
        kernel,
        out_shape=out_shape,
        scratch_shapes=scratch,
        compiler_params=pltpu.CompilerParams(vmem_limit_bytes=VMEM_LIMIT),
        cost_estimate=pl.CostEstimate(flops=cost, bytes_accessed=200000, transcendentals=0),
    )(*args)


def shape(*dims):
    return jax.ShapeDtypeStruct(dims, F32)


def local(
    src_partials,
    att_geom,
    spline_frac,
    cal_partials,
    residual,
    weight,
    source_ids,
    knot_ids,
    ccd_ids,
):
    obs = residual.shape[0]
    tm_count = lax.axis_size("tm")
    z_count = lax.axis_size("src")
    frac, resid, wgt = (x.reshape(1, obs) for x in (spline_frac, residual, weight))
    ids, knots, ccds = (x.reshape(1, obs) for x in (source_ids, knot_ids, ccd_ids))
    send = call(
        pack_kernel,
        shape(tm_count, 8, LANES),
        [pltpu.VMEM((8 * tm_count, obs), BF16), pltpu.VMEM((2, 2 * LANES, obs), BF16)],
        1000000000,
        att_geom,
        frac,
        cal_partials,
        resid,
        wgt,
        knots,
        ccds,
    )
    got = lax.all_to_all(send, "tm", split_axis=0, concat_axis=0, tiled=True)
    src_normal, src_rhs = call(
        source_kernel,
        (shape(5, 5, SRC_DEV), shape(5, SRC_DEV)),
        [pltpu.VMEM((64, obs), BF16)],
        4000000000,
        src_partials,
        resid,
        wgt,
        ids,
    )
    depth = tm_count * 64
    chunks = tm_count * 8 // LANES
    sums = call(
        time_kernel,
        shape(z_count, 72, SEG),
        [
            pltpu.VMEM((chunks, 8 * LANES, LANES), F32),
            pltpu.VMEM((chunks, 8 * LANES, LANES), F32),
            pltpu.VMEM((chunks, 8 * 32, LANES), F32),
            pltpu.VMEM((2 * LANES, depth), BF16),
            pltpu.VMEM((2 * LANES, depth), BF16),
            pltpu.VMEM((64, depth), BF16),
            pltpu.VMEM((SEG, depth), BF16),
            pltpu.VMEM((LANES, depth), BF16),
            pltpu.VMEM((SEG, depth), BF16),
        ],
        1000000000,
        got,
    )
    parts = lax.all_to_all(sums, "src", split_axis=0, concat_axis=0, tiled=True)
    att_normal, att_rhs, cal_normal, cal_rhs = call(
        final_kernel,
        (shape(4, 4, 4, SEG), shape(4, SEG), shape(6, 6, SEG), shape(6, SEG)),
        [pltpu.VMEM((72, SEG), F32)],
        1000000,
        parts,
    )
    return (src_normal, src_rhs, att_normal, att_rhs, cal_normal, cal_rhs)


def solution(mesh):
    both = ("tm", "src")
    in_specs = (
        P(None, both),
        P(None, both),
        P(both),
        P(None, both),
        P(both),
        P(both),
        P(both),
        P(both),
        P(both),
    )
    out_specs = (
        P(None, None, both),
        P(None, both),
        P(None, None, None, "tm"),
        P(None, "tm"),
        P(None, None, "tm"),
        P(None, "tm"),
    )
    return jax.shard_map(local, mesh=mesh, in_specs=in_specs, out_specs=out_specs, check_vma=False)
```

time: 224 us -> 72.6 us (0.32)
  the two profiles are of different devices: /device:TPU:6 before, /device:TPU:1 now
where the time goes in v1:
time: 72.6 us; the launch traced here: 72 us
  blocking collectives  24.9 us (34%)
  waiting for transfers between devices  16.2 us (22%)
  Pallas kernels  14.7 us (20%)
  starting transfers between devices  10.2 us (14%)
  local copies, waits for them, and re-layouts  5.42 us (7%)
    all_to_all x1, blocking collectives, local(): got = lax.all_to_all(send, 'tm', split_axis=0, concat_axis=0, tiled=True)  24.9 us
    all_to_all x1, waiting for transfers between devices, local(): parts = lax.all_to_all(sums, 'src', split_axis=0, concat_axis=0, tiled=True)  16.2 us
    pallas_call x4, Pallas kernels, call(): pl.pallas_call(kernel, out_shape=out_shape, scratch_shapes=scratch, compi...  14.7 us
    all_to_all x1, starting transfers between devices, local(): parts = lax.all_to_all(sums, 'src', split_axis=0, concat_axis=0, tiled=True)  10.2 us
    reshape x6, local copies, waits for them, and re-layouts, local(): x.reshape(1, obs)  4.29 us
  transfers between devices with their start and end apart: 1, of which 1 were waited for; matrix products, arithmetic and copies ran while one was open for 1% of the time, Pallas kernels for 4%

profile of v1, /device:TPU:1, one launch (start us, length us, event | category | flops | bytes accessed | tf_op | source)
XLA Modules:
  0.0 72.0 jit_solution(12223762745790124712)
XLA Ops:
  0.6 0.0 copy-start.1
  0.6 1.3 %reshape.30.resid = f32[1,1536]{1,0:T(1,128)} reshape(f32[1536]{0:T(1024)} %param.13) | data formatting | bytes 12288 | tf_op jit(solution)/shard_map/reshape | solution.py:277
  1.9 0.0 copy-done.1
  1.9 0.0 copy-start.2
  1.9 0.6 reshape.31.weight
  2.5 0.1 copy-done.2
  2.6 0.0 copy-start.3
  2.6 0.6 reshape.33.frac
  3.2 0.1 copy-done.3
  3.3 0.0 copy-start.4
  3.4 0.6 reshape.34.knot
  3.9 0.1 copy-done.4
  4.0 0.6 reshape.35.ccd
  4.6 2.7 %shard_map.137 = f32[64,8,128]{2,1,0:T(8,128)} custom-call(f32[4,1536]{1,0:T(4,128)} %geom.1, f32[1,1536]{1,0:T(1,128)} %reshape.33.frac, f32[6,1536]{1,0:T(8,128)} %cal.1, f32[1,1536]{1,0:T(1,128)} %reshape.30.resid, f32[1,1536]{1,0:T(1,128)} %reshape.31.weight, s32[1,1536]{1,0:T(1,128)} %reshape.34.knot, s32[1,1536]{1,0:T(1,128)} %reshape.35.ccd), custom_call_target="tpu_custom_call" | custom-call | flops 1000000000 | bytes 200000 | tf_op jit(solution)/shard_map/pallas_call | solution.py:250
  7.4 24.9 %all_to_all.10.got = f32[64,8,128]{2,1,0:T(8,128)} all-to-all(f32[64,8,128]{2,1,0:T(8,128)} %shard_map.137), channel_id=1, replica_groups=mesh['tm'=64,'src'=8] {'tm'}, dimensions={0} | all-to-all | bytes 524288 | tf_op jit(solution)/shard_map/all_to_all | solution.py:292
  32.3 7.6 %shard_map.138 = f32[8,72,256]{2,1,0:T(8,128)} custom-call(f32[64,8,128]{2,1,0:T(8,128)} %all_to_all.10.got), custom_call_target="tpu_custom_call" | custom-call | flops 1000000000 | bytes 200000 | tf_op jit(solution)/shard_map/pallas_call | solution.py:250
  39.9 0.0 copy-start.5
  39.9 10.2 %all-to-all-start.1 = ((f32[8,72,256]{2,1,0:T(8,128)}), f32[8,72,256]{2,1,0:T(8,128)S(1)}, u32[]{:S(2)}, u32[]{:S(2)}) async-start(f32[8,72,256]{2,1,0:T(8,128)} %shard_map.138), calls=%async_computation.1 | async-start | bytes 1179648 | tf_op jit(solution)/shard_map/all_to_all | solution.py:322
  50.0 0.0 copy-done.5
  50.0 0.6 reshape.32.ids
  50.6 2.6 %shard_map.136 = (f32[5,5,1024]{2,1,0:T(8,128)}, f32[5,1024]{1,0:T(8,128)}) custom-call(f32[5,1536]{1,0:T(8,128)} %partials.1, f32[1,1536]{1,0:T(1,128)} %reshape.30.resid, f32[1,1536]{1,0:T(1,128)} %reshape.31.weight, s32[1,1536]{1,0:T(1,128)} %reshape.32.ids), custom_call_target="tpu_custom_call" | custom-call | flops 4000000000 | bytes 200000 | tf_op jit(solution)/shard_map/pallas_call | solution.py:250
  53.2 16.2 %all-to-all-done.1.parts = f32[8,72,256]{2,1,0:T(8,128)S(1)} async-done(((f32[8,72,256]{2,1,0:T(8,128)}), f32[8,72,256]{2,1,0:T(8,128)S(1)}, u32[]{:S(2)}, u32[]{:S(2)}) %all-to-all-start.1) | async-done | bytes 589856 | tf_op jit(solution)/shard_map/all_to_all | solution.py:322
  69.4 0.0 copy-start
  69.4 0.8 %copy-done = f32[8,72,256]{2,1,0:T(8,128)} copy-done((f32[8,72,256]{2,1,0:T(8,128)}, f32[8,72,256]{2,1,0:T(8,128)S(1)}, u32[]{:S(2)}) %copy-start) | copy-done | bytes 589848
  70.2 1.8 %shard_map.139 = (f32[4,4,4,256]{3,2,1,0:T(4,128)}, f32[4,256]{1,0:T(4,128)}, f32[6,6,256]{2,1,0:T(8,128)}, f32[6,256]{1,0:T(8,128)}) custom-call(f32[8,72,256]{2,1,0:T(8,128)} %copy-done), custom_call_target="tpu_custom_call" | custom-call | flops 1000000 | bytes 200000 | tf_op jit(solution)/shard_map/pallas_call | solution.py:250
Async XLA Ops:
  0.6 1.3 %copy-start.1 = (f32[1536]{0:T(1024)S(1)}, f32[1536]{0:T(1024)}, u32[]{:S(2)}) copy-start(f32[1536]{0:T(1024)} %param.14) | copy-start | bytes 18436
  1.9 0.7 copy-start.2
  2.6 0.7 copy-start.3
  3.3 0.7 copy-start.4
  39.9 10.2 %copy-start.5 = (s32[1536]{0:T(1024)S(1)}, s32[1536]{0:T(1024)}, u32[]{:S(2)}) copy-start(s32[1536]{0:T(1024)} %param.15) | copy-start | bytes 18436
  39.9 29.5 %all-to-all-start.1 = ((f32[8,72,256]{2,1,0:T(8,128)}), f32[8,72,256]{2,1,0:T(8,128)S(1)}, u32[]{:S(2)}, u32[]{:S(2)}) async-start(f32[8,72,256]{2,1,0:T(8,128)} %shard_map.138), calls=%async_computation.1 | async-start | bytes 1179648 | tf_op jit(solution)/shard_map/all_to_all | solution.py:322
  69.4 0.8 %copy-start = (f32[8,72,256]{2,1,0:T(8,128)}, f32[8,72,256]{2,1,0:T(8,128)S(1)}, u32[]{:S(2)}) copy-start(f32[8,72,256]{2,1,0:T(8,128)S(1)} %all-to-all-done.1.parts) | copy-start | bytes 1769476

commit v2 on v1

v2 whole, which is shorter than its diff:
```python
import jax
import jax.numpy as jnp
from jax import lax
from jax.experimental import pallas as pl
from jax.experimental.pallas import tpu as pltpu
from jax.sharding import PartitionSpec as P

SRC_DEV = 1024
SEG = 256
LANES = 128
F32 = jnp.float32
BF16 = jnp.bfloat16

LOW = 6
FIELDS = 14
HALO_FIELDS = 7
HALO_LANE = LOW * FIELDS
ATT_PAIRS = [(c, e) for c in range(4) for e in range(c, 4)]
CAL_PAIRS = [(p, q) for p in range(6) for q in range(p, 6)]
SRC_PAIRS = [(p, q) for p in range(5) for q in range(p, 5)]
GROUP_ROWS = [48, 40, 24, 16]
GROUP_START = [0, 48, 88, 112]
TERMS = 128
EDGE = TERMS - GROUP_START[1]


def nt_dot(left, right):
    return lax.dot_general(
        left, right, (((1,), (1,)), ((), ())), preferred_element_type=F32
    )


def split(x):
    high = x.astype(BF16)
    return high, (x - high.astype(F32)).astype(BF16)


def onehot(rows, first, ids):
    place = lax.broadcasted_iota(jnp.int32, (rows, ids.shape[1]), 0) + first
    return jnp.where(place == ids, 1.0, 0.0).astype(BF16)


def pack_kernel(*refs):
    count = 7
    hot_s, val_s = refs[count + 1 : count + 3]
    out = refs[count]
    held = refs[count + 3 : -1]
    copies = [
        pltpu.make_async_copy(refs[i], held[i], refs[-1].at[i]) for i in range(count)
    ]
    for copy in copies:
        copy.start()
    for copy in copies:
        copy.wait()
    geom, frac, cal, resid, weight, knot, ccd = held
    obs = knot.shape[0]
    segs = out.shape[0]
    chunk = 256
    blocks = obs // chunk
    knots = knot[...].reshape(1, obs)
    seg = knots // SEG
    member = onehot(segs, 0, seg)
    before = lax.broadcasted_iota(jnp.int32, (chunk, chunk), 0) < lax.broadcasted_iota(
        jnp.int32, (chunk, chunk), 1
    )
    before = jnp.where(before, 1.0, 0.0).astype(BF16)
    counter = jnp.concatenate([before, jnp.ones((chunk, LANES), BF16)], 1)
    carry = jnp.zeros((segs, LANES), F32)
    ranks = []
    for b in range(blocks):
        here = member[:, b * chunk : (b + 1) * chunk]
        counts = jnp.dot(here, counter, preferred_element_type=F32)
        for half in range(chunk // LANES):
            cols = slice(half * LANES, (half + 1) * LANES)
            ranks.append(
                jnp.sum(here[:, cols].astype(F32) * (counts[:, cols] + carry), 0, keepdims=True)
            )
        carry = carry + counts[:, chunk:]
    rank = jnp.concatenate(ranks, 1).astype(jnp.int32)
    high = (rank * 43) >> 8
    low = rank - LOW * high

    wgt = weight[...].reshape(1, obs)
    scale = jnp.sqrt(wgt)
    geoms = geom[...] * scale
    cals = cal[...] * scale
    fields = [geoms[c : c + 1] for c in range(4)]
    fields += [frac[...].reshape(1, obs), resid[...].reshape(1, obs) * scale]
    fields += [(knots - SEG * seg).astype(F32)]
    fields += [cals[p : p + 1] for p in range(6)]
    fields += [ccd[...].reshape(1, obs).astype(F32)]
    fields = jnp.concatenate(fields, 0)
    rounded = fields.astype(BF16).astype(F32)
    parts = (rounded, fields - rounded)
    sub = lax.broadcasted_iota(jnp.int32, (8, obs), 0)
    masks = [(sub + 8 * j) % LOW == low for j in range(3)]
    for i, part in enumerate(parts):
        tiles = []
        for j in range(LANES // 8):
            first, last = 8 * j // LOW, (8 * j + 7) // LOW
            if first >= FIELDS:
                tiles.append(jnp.zeros((8, obs), F32))
                continue
            value = jnp.broadcast_to(part[first : first + 1], (8, obs))
            for f in range(first + 1, last + 1):
                row = part[f : f + 1] if f < FIELDS else 0.0
                value = jnp.where(sub < LOW * f - 8 * j, value, row)
            tiles.append(jnp.where(masks[j % 3], value, 0.0))
        for j in range(0, LANES // 8, 2):
            at = i * LANES + 8 * j
            val_s[at : at + 16, :] = jnp.concatenate(tiles[j : j + 2], 0).astype(BF16)
    code = seg * 8 + high
    for j in range(0, 8 * segs, 64):
        hot_s[j : j + 64, :] = onehot(64, j, code)
    main = nt_dot(hot_s[...], val_s[...])
    main = main[:, :LANES] + main[:, LANES:]
    lane = lax.broadcasted_iota(jnp.int32, (8 * segs, LANES), 1)
    shifted = jnp.concatenate([jnp.zeros((8, LANES), F32), main[:-8]], 0)
    shifted = pltpu.roll(shifted, HALO_LANE, 1)
    out[...] = jnp.where(lane < HALO_LANE, main, shifted).reshape(segs, 8, LANES)


def source_kernel(partials, resid, weight, ids, normal, rhs, left_s):
    obs = ids.shape[0]
    wgt, res, idv = (x[...].reshape(1, obs) for x in (weight, resid, ids))
    count = partials.shape[0]
    part = partials[...]
    rows = [part[p : p + 1] for p in range(count)]
    scaled = part * wgt
    scaled_rows = [scaled[p : p + 1] for p in range(count)]
    terms = [scaled_rows[p] * rows[q] for p, q in SRC_PAIRS]
    terms += [scaled_rows[p] * res for p in range(count)]
    terms += [jnp.zeros((32 - len(terms), obs), F32)]
    high, low = split(jnp.concatenate(terms, 0))
    left_s[0:32, :] = high
    left_s[32:64, :] = low
    left = left_s[...]
    step = 256
    for j in range(0, SRC_DEV, step):
        sums = nt_dot(left, onehot(step, j, idv))
        sums = sums[:32] + sums[32:]
        for t, (p, q) in enumerate(SRC_PAIRS):
            normal[p, q : q + 1, j : j + step] = sums[t : t + 1]
            if p != q:
                normal[q, p : p + 1, j : j + step] = sums[t : t + 1]
        rhs[:, j : j + step] = sums[len(SRC_PAIRS) : len(SRC_PAIRS) + count]


def att_terms(rows, first):
    geoms = rows[:4]
    frac, resid = rows[4], rows[5]
    remain = 1.0 - frac
    square = frac * frac
    cubic = square * frac
    basis = [
        remain * remain * remain * (1.0 / 6.0),
        (3.0 * cubic - 6.0 * square + 4.0) * (1.0 / 6.0),
        (-3.0 * cubic + 3.0 * square + 3.0 * frac + 1.0) * (1.0 / 6.0),
        cubic * (1.0 / 6.0),
    ]
    pairs = [geoms[c] * geoms[e] for c, e in ATT_PAIRS]
    weighted = [geoms[c] * resid for c in range(4)]
    terms = []
    for a in range(first, 4):
        place = GROUP_START[a]
        for c in range(4):
            terms.append((place + c, basis[a] * weighted[c]))
        place = place + 4
        for d in range(4 - a):
            both = basis[a] * basis[a + d]
            for q in range(10):
                terms.append((place + q, both * pairs[q]))
            place = place + 10
        for t in range(place, GROUP_START[a] + GROUP_ROWS[a]):
            terms.append((t, jnp.zeros_like(frac)))
    return terms


def time_kernel(got, out, turned_s, att_f, halo_f, cal_f, att_l, halo_l, cal_l, knot_hot, halo_hot, ccd_hot):
    chunks = got.shape[0] * 8 // LANES
    for c in range(chunks):
        turned_s[c] = got[c * 16 : (c + 1) * 16].reshape(LANES, LANES).T
        rows = [turned_s[c, LOW * f : LOW * f + LOW, :] for f in range(FIELDS + HALO_FIELDS)]
        for t, value in att_terms(rows, 0):
            att_f[c, pl.ds(t, LOW, stride=TERMS), :] = value
        cals = rows[7:13]
        terms = [cals[p] * cals[q] for p, q in CAL_PAIRS]
        terms += [cals[p] * rows[5] for p in range(6)]
        terms += [jnp.zeros((LOW, LANES), F32)] * (32 - len(terms))
        for t, value in enumerate(terms):
            cal_f[c, pl.ds(t, LOW, stride=32), :] = value
        for t, value in att_terms(rows[FIELDS:], 1):
            halo_f[c, pl.ds(t - GROUP_START[1], LOW, stride=EDGE), :] = value
        for l in range(LOW):
            at = (c * LOW + l) * LANES
            cols = slice(at, at + LANES)
            att_l[0:TERMS, cols], att_l[TERMS:, cols] = split(att_f[c, l * TERMS : (l + 1) * TERMS, :])
            halo_l[0:EDGE, cols], halo_l[EDGE:, cols] = split(halo_f[c, l * EDGE : (l + 1) * EDGE, :])
            cal_l[0:32, cols], cal_l[32:, cols] = split(cal_f[c, l * 32 : (l + 1) * 32, :])

            def label(f):
                return turned_s[c, LOW * f + l : LOW * f + l + 1, :].astype(jnp.int32)

            knot_hot[:, cols] = onehot(SEG, 0, label(6))
            ccd_hot[:, cols] = onehot(SEG, 0, label(13))
            halo_hot[:, cols] = onehot(16, SEG - 16, label(FIELDS + 6))
    main = nt_dot(att_l[...], knot_hot[...])
    main = main[:TERMS] + main[TERMS:]
    edge = nt_dot(halo_l[...], halo_hot[...])
    edge = edge[:EDGE] + edge[EDGE:]
    edge = jnp.concatenate([jnp.zeros((EDGE, LANES - 16), F32), edge], 1)
    total = main[: GROUP_ROWS[0]]
    for a in range(1, 4):
        n = GROUP_ROWS[a]
        at = GROUP_START[a]
        group = jnp.concatenate([edge[at - GROUP_START[1] :][:n], main[at : at + n]], 1)
        group = pltpu.roll(group, a, 1)[:, LANES:]
        if n < GROUP_ROWS[0]:
            group = jnp.concatenate([group, jnp.zeros((GROUP_ROWS[0] - n, SEG), F32)], 0)
        total = total + group
    cal = nt_dot(cal_l[...], ccd_hot[...])
    cal = cal[:32] + cal[32:]
    for z in range(out.shape[0]):
        out[z, 0:48, :] = total
        out[z, 48:72, :] = cal[0:24]
        out[z, 44:47, :] = cal[24:27]


def final_kernel(parts, att_normal, att_rhs, cal_normal, cal_rhs, sum_s):
    total = parts[0]
    for z in range(1, parts.shape[0]):
        total = total + parts[z]
    sum_s[...] = total
    att_rhs[...] = sum_s[0:4, :]
    for d in range(4):
        for q, (c, e) in enumerate(ATT_PAIRS):
            row = sum_s[4 + 10 * d + q : 5 + 10 * d + q, :]
            att_normal[d, c, e : e + 1, :] = row
            if c != e:
                att_normal[d, e, c : c + 1, :] = row

    def cal_row(t):
        at = 48 + t if t < 24 else 20 + t
        return sum_s[at : at + 1, :]

    for t, (p, q) in enumerate(CAL_PAIRS):
        cal_normal[p, q : q + 1, :] = cal_row(t)
        if p != q:
            cal_normal[q, p : p + 1, :] = cal_row(t)
    for p in range(6):
        cal_rhs[p : p + 1, :] = cal_row(21 + p)


def call(kernel, out_shape, scratch, vmem_mib, cost, *args, space=pltpu.VMEM):
    return pl.pallas_call(
        kernel,
        out_shape=out_shape,
        in_specs=[pl.BlockSpec(memory_space=space)] * len(args),
        scratch_shapes=scratch,
        compiler_params=pltpu.CompilerParams(vmem_limit_bytes=vmem_mib * 1024 * 1024),
        cost_estimate=pl.CostEstimate(flops=cost, bytes_accessed=200000, transcendentals=0),
    )(*args)


def shape(*dims):
    return jax.ShapeDtypeStruct(dims, F32)


def local(
    src_partials,
    att_geom,
    spline_frac,
    cal_partials,
    residual,
    weight,
    source_ids,
    knot_ids,
    ccd_ids,
):
    obs = residual.shape[0]
    tm_count = lax.axis_size("tm")
    z_count = lax.axis_size("src")
    rows = (att_geom, spline_frac, cal_partials, residual, weight, knot_ids, ccd_ids)
    send = call(
        pack_kernel,
        shape(tm_count, 8, LANES),
        [pltpu.VMEM((8 * tm_count, obs), BF16), pltpu.VMEM((2 * LANES, obs), BF16)]
        + [pltpu.VMEM(x.shape, x.dtype) for x in rows]
        + [pltpu.SemaphoreType.DMA((len(rows),))],
        12,
        1000000000,
        *rows,
        space=pltpu.HBM,
    )
    got = lax.all_to_all(send, "tm", split_axis=0, concat_axis=0, tiled=True)
    src_normal, src_rhs = call(
        source_kernel,
        (shape(5, 5, SRC_DEV), shape(5, SRC_DEV)),
        [pltpu.VMEM((64, obs), BF16)],
        12,
        4000000000,
        src_partials,
        residual,
        weight,
        source_ids,
    )
    chunks = tm_count * 8 // LANES
    depth = chunks * LOW * LANES
    sums = call(
        time_kernel,
        shape(z_count, 72, SEG),
        [
            pltpu.VMEM((chunks, LANES, LANES), F32),
            pltpu.VMEM((chunks, LOW * TERMS, LANES), F32),
            pltpu.VMEM((chunks, LOW * EDGE, LANES), F32),
            pltpu.VMEM((chunks, LOW * 32, LANES), F32),
            pltpu.VMEM((2 * TERMS, depth), BF16),
            pltpu.VMEM((2 * EDGE, depth), BF16),
            pltpu.VMEM((64, depth), BF16),
            pltpu.VMEM((SEG, depth), BF16),
            pltpu.VMEM((16, depth), BF16),
            pltpu.VMEM((SEG, depth), BF16),
        ],
        24,
        1000000000,
        got,
    )
    parts = lax.all_to_all(sums, "src", split_axis=0, concat_axis=0, tiled=True)
    att_normal, att_rhs, cal_normal, cal_rhs = call(
        final_kernel,
        (shape(4, 4, 4, SEG), shape(4, SEG), shape(6, 6, SEG), shape(6, SEG)),
        [pltpu.VMEM((72, SEG), F32)],
        8,
        1000000,
        parts,
    )
    return (src_normal, src_rhs, att_normal, att_rhs, cal_normal, cal_rhs)


def solution(mesh):
    both = ("tm", "src")
    in_specs = (
        P(None, both),
        P(None, both),
        P(both),
        P(None, both),
        P(both),
        P(both),
        P(both),
        P(both),
        P(both),
    )
    out_specs = (
        P(None, None, both),
        P(None, both),
        P(None, None, None, "tm"),
        P(None, "tm"),
        P(None, None, "tm"),
        P(None, "tm"),
    )
    return jax.shard_map(local, mesh=mesh, in_specs=in_specs, out_specs=out_specs, check_vma=False)
```

time: 72.6 us -> 66.6 us (0.917)
  Pallas kernels: 14.7 us -> 8 us
  waiting for transfers between devices: 16.2 us -> 17.6 us
    pallas_call x4, Pallas kernels: 14.7 us -> 8 us  [call(): pl.pallas_call(kernel, out_shape=out_shape, in_specs=[pl.BlockSpec(memory...]
    reshape x6 -> x0, local copies, waits for them, and re-layouts: 4.29 us -> none  [local(): x.reshape(1, obs)]
    unnamed x12 -> x22, local copies, waits for them, and re-layouts: 1.13 us -> 5.02 us
    all_to_all x1, waiting for transfers between devices: 16.2 us -> 17.6 us  [local(): parts = lax.all_to_all(sums, 'src', split_axis=0, concat_axis=0, tiled=True)]
  transfers between devices with their start and end apart: 1 -> 1, of which waited for: 1 -> 1; matrix products, arithmetic and copies ran while one was open for 1% -> 0% of each run, Pallas kernels for 4% -> 3%
where the time goes in v2:
time: 66.6 us; the launch traced here: 66.1 us
  blocking collectives  24.6 us (37%)
  waiting for transfers between devices  17.6 us (26%)
  starting transfers between devices  10.2 us (15%)
  Pallas kernels  8 us (12%)
  local copies, waits for them, and re-layouts  5.02 us (8%)
  between operations  0.69 us (1%)
    all_to_all x1, blocking collectives, local(): got = lax.all_to_all(send, 'tm', split_axis=0, concat_axis=0, tiled=True)  24.6 us
    all_to_all x1, waiting for transfers between devices, local(): parts = lax.all_to_all(sums, 'src', split_axis=0, concat_axis=0, tiled=True)  17.6 us
    all_to_all x1, starting transfers between devices, local(): parts = lax.all_to_all(sums, 'src', split_axis=0, concat_axis=0, tiled=True)  10.2 us
    pallas_call x4, Pallas kernels, call(): pl.pallas_call(kernel, out_shape=out_shape, in_specs=[pl.BlockSpec(memory...  8 us
    unnamed x22, local copies, waits for them, and re-layouts  5.02 us
  transfers between devices with their start and end apart: 1, of which 1 were waited for; matrix products, arithmetic and copies ran while one was open for 0% of the time, Pallas kernels for 3%

profile of v2, /device:TPU:1, one launch (start us, length us, event | category | flops | bytes accessed | tf_op | source)
XLA Modules:
  0.0 66.1 jit_solution(14799837662680421293)
XLA Ops:
  0.6 0.0 copy-start
  0.6 0.8 %copy-done = f32[6,1536]{1,0:T(8,128)S(1)} copy-done((f32[6,1536]{1,0:T(8,128)S(1)}, f32[6,1536]{1,0:T(8,128)}, u32[]{:S(2)}) %copy-start) | copy-done | bytes 36888
  1.4 0.0 copy-start.2
  1.4 0.7 %copy-done.2 = f32[4,1536]{1,0:T(4,128)S(1)} copy-done((f32[4,1536]{1,0:T(4,128)S(1)}, f32[4,1536]{1,0:T(4,128)}, u32[]{:S(2)}) %copy-start.2) | copy-done | bytes 24600
  2.2 0.0 copy-start.3
  2.2 0.7 %copy-done.3 = f32[1536]{0:T(1024)S(1)} copy-done((f32[1536]{0:T(1024)S(1)}, f32[1536]{0:T(1024)}, u32[]{:S(2)}) %copy-start.3) | copy-done | bytes 6168
  2.9 0.0 copy-start.4
  2.9 0.7 %copy-done.4 = s32[1536]{0:T(1024)S(1)} copy-done((s32[1536]{0:T(1024)S(1)}, s32[1536]{0:T(1024)}, u32[]{:S(2)}) %copy-start.4) | copy-done | bytes 6168
  3.6 0.0 copy-start.5
  3.6 0.7 %copy-done.5 = s32[1536]{0:T(1024)S(1)} copy-done((s32[1536]{0:T(1024)S(1)}, s32[1536]{0:T(1024)}, u32[]{:S(2)}) %copy-start.5) | copy-done | bytes 6168
  4.3 0.0 copy-start.6
  4.3 0.7 %copy-done.6 = f32[1536]{0:T(1024)S(1)} copy-done((f32[1536]{0:T(1024)S(1)}, f32[1536]{0:T(1024)}, u32[]{:S(2)}) %copy-start.6) | copy-done | bytes 6168
  5.0 0.0 copy-start.8
  5.0 0.7 %copy-done.8 = f32[1536]{0:T(1024)S(1)} copy-done((f32[1536]{0:T(1024)S(1)}, f32[1536]{0:T(1024)}, u32[]{:S(2)}) %copy-start.8) | copy-done | bytes 6168
  5.7 1.1 %shard_map.137 = f32[64,8,128]{2,1,0:T(8,128)S(1)} custom-call(f32[4,1536]{1,0:T(4,128)S(1)} %copy-done.2, f32[1536]{0:T(1024)S(1)} %copy-done.3, f32[6,1536]{1,0:T(8,128)S(1)} %copy-done, f32[1536]{0:T(1024)S(1)} %copy-done.6, f32[1536]{0:T(1024)S(1)} %copy-done.8, s32[1536]{0:T(1024)S(1)} %copy-done.4, s32[1536]{0:T(1024)S(1)} %copy-done.5), custom_call_target="tpu_custom_call" | custom-call | flops 1000000000 | bytes 200000 | tf_op jit(solution)/shard_map/pallas_call | solution.py:255
  6.8 24.6 %all_to_all.10.got = f32[64,8,128]{2,1,0:T(8,128)S(1)} all-to-all(f32[64,8,128]{2,1,0:T(8,128)S(1)} %shard_map.137), channel_id=1, replica_groups=mesh['tm'=64,'src'=8] {'tm'}, dimensions={0} | all-to-all | bytes 524288 | tf_op jit(solution)/shard_map/all_to_all | solution.py:295
  31.4 4.4 %shard_map.138 = f32[8,72,256]{2,1,0:T(8,128)} custom-call(f32[64,8,128]{2,1,0:T(8,128)S(1)} %all_to_all.10.got), custom_call_target="tpu_custom_call" | custom-call | flops 1000000000 | bytes 200000 | tf_op jit(solution)/shard_map/pallas_call | solution.py:255
  35.8 0.0 copy-start.1
  35.8 0.0 copy-start.7
  35.8 0.0 copy-start.9
  35.8 0.0 copy-start.10
  35.8 10.2 %all-to-all-start.1 = ((f32[8,72,256]{2,1,0:T(8,128)}), f32[8,72,256]{2,1,0:T(8,128)S(1)}, u32[]{:S(2)}, u32[]{:S(2)}) async-start(f32[8,72,256]{2,1,0:T(8,128)} %shard_map.138), calls=%async_computation.1 | async-start | bytes 1179648 | tf_op jit(solution)/shard_map/all_to_all | solution.py:328
  46.0 0.0 copy-done.1
  46.0 0.0 copy-done.7
  46.0 0.0 copy-done.9
  46.0 0.0 copy-done.10
  46.0 1.8 %shard_map.136 = (f32[5,5,1024]{2,1,0:T(8,128)}, f32[5,1024]{1,0:T(8,128)}) custom-call(f32[5,1536]{1,0:T(8,128)S(1)} %copy-done.1, f32[1536]{0:T(1024)S(1)} %copy-done.7, f32[1536]{0:T(1024)S(1)} %copy-done.9, s32[1536]{0:T(1024)S(1)} %copy-done.10), custom_call_target="tpu_custom_call" | custom-call | flops 4000000000 | bytes 200000 | tf_op jit(solution)/shard_map/pallas_call | solution.py:255
  47.8 17.6 %all-to-all-done.1.parts = f32[8,72,256]{2,1,0:T(8,128)S(1)} async-done(((f32[8,72,256]{2,1,0:T(8,128)}), f32[8,72,256]{2,1,0:T(8,128)S(1)}, u32[]{:S(2)}, u32[]{:S(2)}) %all-to-all-start.1) | async-done | bytes 589856 | tf_op jit(solution)/shard_map/all_to_all | solution.py:328
  65.3 0.7 %shard_map.139 = (f32[4,4,4,256]{3,2,1,0:T(4,128)}, f32[4,256]{1,0:T(4,128)}, f32[6,6,256]{2,1,0:T(8,128)}, f32[6,256]{1,0:T(8,128)}) custom-call(f32[8,72,256]{2,1,0:T(8,128)S(1)} %all-to-all-done.1.parts), custom_call_target="tpu_custom_call" | custom-call | flops 1000000 | bytes 200000 | tf_op jit(solution)/shard_map/pallas_call | solution.py:255
Async XLA Ops:
  0.6 0.8 %copy-start = (f32[6,1536]{1,0:T(8,128)S(1)}, f32[6,1536]{1,0:T(8,128)}, u32[]{:S(2)}) copy-start(f32[6,1536]{1,0:T(8,128)} %refs_2_.1) | copy-start | bytes 110596
  1.4 0.7 %copy-start.2 = (f32[4,1536]{1,0:T(4,128)S(1)}, f32[4,1536]{1,0:T(4,128)}, u32[]{:S(2)}) copy-start(f32[4,1536]{1,0:T(4,128)} %refs_0_.1) | copy-start | bytes 73732
  2.2 0.7 %copy-start.3 = (f32[1536]{0:T(1024)S(1)}, f32[1536]{0:T(1024)}, u32[]{:S(2)}) copy-start(f32[1536]{0:T(1024)} %refs_1_.1) | copy-start | bytes 18436
  2.9 0.7 %copy-start.4 = (s32[1536]{0:T(1024)S(1)}, s32[1536]{0:T(1024)}, u32[]{:S(2)}) copy-start(s32[1536]{0:T(1024)} %refs_5_.1) | copy-start | bytes 18436
  3.6 0.7 %copy-start.5 = (s32[1536]{0:T(1024)S(1)}, s32[1536]{0:T(1024)}, u32[]{:S(2)}) copy-start(s32[1536]{0:T(1024)} %refs_6_.1) | copy-start | bytes 18436
  4.3 0.7 %copy-start.6 = (f32[1536]{0:T(1024)S(1)}, f32[1536]{0:T(1024)}, u32[]{:S(2)}) copy-start(f32[1536]{0:T(1024)} %refs_3_.1) | copy-start | bytes 18436
  5.0 0.7 %copy-start.8 = (f32[1536]{0:T(1024)S(1)}, f32[1536]{0:T(1024)}, u32[]{:S(2)}) copy-start(f32[1536]{0:T(1024)} %refs_4_.1) | copy-start | bytes 18436
  35.8 10.2 %copy-start.1 = (f32[5,1536]{1,0:T(8,128)S(1)}, f32[5,1536]{1,0:T(8,128)}, u32[]{:S(2)}) copy-start(f32[5,1536]{1,0:T(8,128)} %partials.1) | copy-start | bytes 92164
  35.8 10.2 %copy-start.7 = (f32[1536]{0:T(1024)S(1)}, f32[1536]{0:T(1024)}, u32[]{:S(2)}) copy-start(f32[1536]{0:T(1024)} %refs_3_.1) | copy-start | bytes 18436
  35.8 10.2 %copy-start.9 = (f32[1536]{0:T(1024)S(1)}, f32[1536]{0:T(1024)}, u32[]{:S(2)}) copy-start(f32[1536]{0:T(1024)} %refs_4_.1) | copy-start | bytes 18436
  35.8 10.2 %copy-start.10 = (s32[1536]{0:T(1024)S(1)}, s32[1536]{0:T(1024)}, u32[]{:S(2)}) copy-start(s32[1536]{0:T(1024)} %ids.1) | copy-start | bytes 18436
  35.8 29.6 %all-to-all-start.1 = ((f32[8,72,256]{2,1,0:T(8,128)}), f32[8,72,256]{2,1,0:T(8,128)S(1)}, u32[]{:S(2)}, u32[]{:S(2)}) async-start(f32[8,72,256]{2,1,0:T(8,128)} %shard_map.138), calls=%async_computation.1 | async-start | bytes 1179648 | tf_op jit(solution)/shard_map/all_to_all | solution.py:328

commit v3 on v2

--- a/solution.py
+++ b/solution.py
@@ -21,6 +21,7 @@
 GROUP_ROWS = [48, 40, 24, 16]
 GROUP_START = [0, 48, 88, 112]
 TERMS = 128
+PACK_MIB = 56
 EDGE = TERMS - GROUP_START[1]
 
 
@@ -48,11 +49,10 @@
     copies = [
         pltpu.make_async_copy(refs[i], held[i], refs[-1].at[i]) for i in range(count)
     ]
-    for copy in copies:
-        copy.start()
-    for copy in copies:
-        copy.wait()
+    for i in (5, 0, 1, 2, 3, 4, 6):
+        copies[i].start()
     geom, frac, cal, resid, weight, knot, ccd = held
+    copies[5].wait()
     obs = knot.shape[0]
     segs = out.shape[0]
     chunk = 256
@@ -80,8 +80,9 @@
     high = (rank * 43) >> 8
     low = rank - LOW * high
 
-    wgt = weight[...].reshape(1, obs)
-    scale = jnp.sqrt(wgt)
+    for i in (0, 1, 2, 3, 4, 6):
+        copies[i].wait()
+    scale = jnp.sqrt(weight[...].reshape(1, obs))
     geoms = geom[...] * scale
     cals = cal[...] * scale
     fields = [geoms[c : c + 1] for c in range(4)]
@@ -287,7 +288,7 @@
         [pltpu.VMEM((8 * tm_count, obs), BF16), pltpu.VMEM((2 * LANES, obs), BF16)]
         + [pltpu.VMEM(x.shape, x.dtype) for x in rows]
         + [pltpu.SemaphoreType.DMA((len(rows),))],
-        12,
+        PACK_MIB,
         1000000000,
         *rows,
         space=pltpu.HBM,
@@ -304,6 +305,7 @@
         weight,
         source_ids,
     )
+    got, src_normal, src_rhs = lax.optimization_barrier((got, src_normal, src_rhs))
     chunks = tm_count * 8 // LANES
     depth = chunks * LOW * LANES
     sums = call(

time: 66.6 us -> 60.9 us (0.914)
  waiting for transfers between devices: 17.6 us -> 11.4 us
  local copies, waits for them, and re-layouts: 5.02 us -> 0.03 us
  blocking collectives: 24.6 us -> 28.3 us
  starting transfers between devices: 10.2 us -> 11.8 us
    all_to_all x1, waiting for transfers between devices: 17.6 us -> 11.4 us  [local(): got = lax.all_to_all(send, 'tm', split_axis=0, concat_axis=0, tiled=True)]
    unnamed x22 -> x8, local copies, waits for them, and re-layouts: 5.02 us -> 0.03 us
    all_to_all x1, blocking collectives: 24.6 us -> 28.3 us  [local(): parts = lax.all_to_all(sums, 'src', split_axis=0, concat_axis=0, tiled=True)]
    all_to_all x1, starting transfers between devices: 10.2 us -> 11.8 us  [local(): got = lax.all_to_all(send, 'tm', split_axis=0, concat_axis=0, tiled=True)]
where the time goes in v3:
time: 60.9 us; the launch traced here: 60.7 us
  blocking collectives  28.3 us (46%)
  starting transfers between devices  11.8 us (19%)
  waiting for transfers between devices  11.4 us (19%)
  Pallas kernels  8.54 us (14%)
  between operations  0.72 us (1%)
    all_to_all x1, blocking collectives, local(): parts = lax.all_to_all(sums, 'src', split_axis=0, concat_axis=0, tiled=True)  28.3 us
    all_to_all x1, starting transfers between devices, local(): got = lax.all_to_all(send, 'tm', split_axis=0, concat_axis=0, tiled=True)  11.8 us
    all_to_all x1, waiting for transfers between devices, local(): got = lax.all_to_all(send, 'tm', split_axis=0, concat_axis=0, tiled=True)  11.4 us
    pallas_call x4, Pallas kernels, call(): pl.pallas_call(kernel, out_shape=out_shape, in_specs=[pl.BlockSpec(memory...  8.54 us
  transfers between devices with their start and end apart: 1, of which 1 were waited for; matrix products, arithmetic and copies ran while one was open for 0% of the time, Pallas kernels for 3%

profile of v3, /device:TPU:1, one launch (start us, length us, event | category | flops | bytes accessed | tf_op | source)
XLA Modules:
  0.0 60.7 jit_solution(18381855560146885703)
XLA Ops:
  0.6 2.5 %shard_map.136 = f32[64,8,128]{2,1,0:T(8,128)} custom-call(f32[4,1536]{1,0:T(4,128)} %refs_0_.1, f32[1536]{0:T(1024)} %refs_1_.1, f32[6,1536]{1,0:T(8,128)} %refs_2_.1, f32[1536]{0:T(1024)} %resid.1, f32[1536]{0:T(1024)} %weight.1, s32[1536]{0:T(1024)} %refs_5_.1, s32[1536]{0:T(1024)} %refs_6_.1), custom_call_target="tpu_custom_call" | custom-call | flops 1000000000 | bytes 200000 | tf_op jit(solution)/shard_map/pallas_call | solution.py:256
  3.1 0.0 copy-start
  3.2 0.0 copy-start.1
  3.2 0.0 copy-start.2
  3.2 0.0 copy-start.3
  3.2 11.8 %all-to-all-start = ((f32[64,8,128]{2,1,0:T(8,128)}), f32[64,8,128]{2,1,0:T(8,128)S(1)}, u32[]{:S(2)}, u32[]{:S(2)}) async-start(f32[64,8,128]{2,1,0:T(8,128)} %shard_map.136), calls=%async_computation | async-start | bytes 524288 | tf_op jit(solution)/shard_map/all_to_all | solution.py:296
  15.0 0.0 copy-done
  15.0 0.0 copy-done.1
  15.0 0.0 copy-done.2
  15.0 0.0 copy-done.3
  15.0 1.8 %shard_map.137 = (f32[5,5,1024]{2,1,0:T(8,128)}, f32[5,1024]{1,0:T(8,128)}) custom-call(f32[5,1536]{1,0:T(8,128)S(1)} %copy-done, f32[1536]{0:T(1024)S(1)} %copy-done.1, f32[1536]{0:T(1024)S(1)} %copy-done.2, s32[1536]{0:T(1024)S(1)} %copy-done.3), custom_call_target="tpu_custom_call" | custom-call | flops 4000000000 | bytes 200000 | tf_op jit(solution)/shard_map/pallas_call | solution.py:256
  16.8 11.4 %all-to-all-done.got = f32[64,8,128]{2,1,0:T(8,128)S(1)} async-done(((f32[64,8,128]{2,1,0:T(8,128)}), f32[64,8,128]{2,1,0:T(8,128)S(1)}, u32[]{:S(2)}, u32[]{:S(2)}) %all-to-all-start) | async-done | bytes 262176 | tf_op jit(solution)/shard_map/all_to_all | solution.py:296
  28.1 3.5 %shard_map.138 = f32[8,72,256]{2,1,0:T(8,128)S(1)} custom-call(f32[64,8,128]{2,1,0:T(8,128)S(1)} %all-to-all-done.got), custom_call_target="tpu_custom_call" | custom-call | flops 1000000000 | bytes 200000 | tf_op jit(solution)/shard_map/pallas_call | solution.py:256
  31.7 28.3 %all_to_all.10.parts = f32[8,72,256]{2,1,0:T(8,128)S(1)} all-to-all(f32[8,72,256]{2,1,0:T(8,128)S(1)} %shard_map.138), channel_id=1, replica_groups=mesh['tm'=64,'src'=8] {'src'}, dimensions={0} | all-to-all | bytes 1179648 | tf_op jit(solution)/shard_map/all_to_all | solution.py:330
  59.9 0.7 %shard_map.139 = (f32[4,4,4,256]{3,2,1,0:T(4,128)}, f32[4,256]{1,0:T(4,128)}, f32[6,6,256]{2,1,0:T(8,128)}, f32[6,256]{1,0:T(8,128)}) custom-call(f32[8,72,256]{2,1,0:T(8,128)S(1)} %all_to_all.10.parts), custom_call_target="tpu_custom_call" | custom-call | flops 1000000 | bytes 200000 | tf_op jit(solution)/shard_map/pallas_call | solution.py:256
Async XLA Ops:
  3.1 11.8 %copy-start = (f32[5,1536]{1,0:T(8,128)S(1)}, f32[5,1536]{1,0:T(8,128)}, u32[]{:S(2)}) copy-start(f32[5,1536]{1,0:T(8,128)} %partials.1) | copy-start | bytes 92164
  3.2 11.8 %copy-start.1 = (f32[1536]{0:T(1024)S(1)}, f32[1536]{0:T(1024)}, u32[]{:S(2)}) copy-start(f32[1536]{0:T(1024)} %resid.1) | copy-start | bytes 18436
  3.2 11.8 %copy-start.2 = (f32[1536]{0:T(1024)S(1)}, f32[1536]{0:T(1024)}, u32[]{:S(2)}) copy-start(f32[1536]{0:T(1024)} %weight.1) | copy-start | bytes 18436
  3.2 11.8 %copy-start.3 = (s32[1536]{0:T(1024)S(1)}, s32[1536]{0:T(1024)}, u32[]{:S(2)}) copy-start(s32[1536]{0:T(1024)} %ids.1) | copy-start | bytes 18436
  3.2 24.9 %all-to-all-start = ((f32[64,8,128]{2,1,0:T(8,128)}), f32[64,8,128]{2,1,0:T(8,128)S(1)}, u32[]{:S(2)}, u32[]{:S(2)}) async-start(f32[64,8,128]{2,1,0:T(8,128)} %shard_map.136), calls=%async_computation | async-start | bytes 524288 | tf_op jit(solution)/shard_map/all_to_all | solution.py:296

commit v4 on v3

--- a/solution.py
+++ b/solution.py
@@ -23,6 +23,7 @@
 TERMS = 128
 PACK_MIB = 56
 EDGE = TERMS - GROUP_START[1]
+TERMS_STEP, EDGE_STEP, CAL_STEP = TERMS + 1, EDGE + 1, 32 + 1
 
 
 def nt_dot(left, right):
@@ -39,6 +40,12 @@
 def onehot(rows, first, ids):
     place = lax.broadcasted_iota(jnp.int32, (rows, ids.shape[1]), 0) + first
     return jnp.where(place == ids, 1.0, 0.0).astype(BF16)
+
+
+def label_hot(rows, first, ids):
+    place = (lax.broadcasted_iota(jnp.int32, (rows, ids.shape[1]), 0) + first).astype(F32).astype(BF16)
+    same = place == jnp.broadcast_to(ids, place.shape).astype(BF16)
+    return jnp.where(same, jnp.ones_like(place), jnp.zeros_like(place))
 
 
 def pack_kernel(*refs):
@@ -59,7 +66,7 @@
     blocks = obs // chunk
     knots = knot[...].reshape(1, obs)
     seg = knots // SEG
-    member = onehot(segs, 0, seg)
+    member = label_hot(segs, 0, seg.astype(F32))
     before = lax.broadcasted_iota(jnp.int32, (chunk, chunk), 0) < lax.broadcasted_iota(
         jnp.int32, (chunk, chunk), 1
     )
@@ -112,7 +119,7 @@
             val_s[at : at + 16, :] = jnp.concatenate(tiles[j : j + 2], 0).astype(BF16)
     code = seg * 8 + high
     for j in range(0, 8 * segs, 64):
-        hot_s[j : j + 64, :] = onehot(64, j, code)
+        hot_s[j : j + 64, :] = label_hot(64, 0, (code - j).astype(F32))
     main = nt_dot(hot_s[...], val_s[...])
     main = main[:, :LANES] + main[:, LANES:]
     lane = lax.broadcasted_iota(jnp.int32, (8 * segs, LANES), 1)
@@ -183,31 +190,36 @@
         turned_s[c] = got[c * 16 : (c + 1) * 16].reshape(LANES, LANES).T
         rows = [turned_s[c, LOW * f : LOW * f + LOW, :] for f in range(FIELDS + HALO_FIELDS)]
         for t, value in att_terms(rows, 0):
-            att_f[c, pl.ds(t, LOW, stride=TERMS), :] = value
+            att_f[c, pl.ds(t, LOW, stride=TERMS_STEP), :] = value
         cals = rows[7:13]
         terms = [cals[p] * cals[q] for p, q in CAL_PAIRS]
         terms += [cals[p] * rows[5] for p in range(6)]
         terms += [jnp.zeros((LOW, LANES), F32)] * (32 - len(terms))
         for t, value in enumerate(terms):
-            cal_f[c, pl.ds(t, LOW, stride=32), :] = value
+            cal_f[c, pl.ds(t, LOW, stride=CAL_STEP), :] = value
         for t, value in att_terms(rows[FIELDS:], 1):
-            halo_f[c, pl.ds(t - GROUP_START[1], LOW, stride=EDGE), :] = value
+            halo_f[c, pl.ds(t - GROUP_START[1], LOW, stride=EDGE_STEP), :] = value
         for l in range(LOW):
-            at = (c * LOW + l) * LANES
+            at = l * LANES
             cols = slice(at, at + LANES)
-            att_l[0:TERMS, cols], att_l[TERMS:, cols] = split(att_f[c, l * TERMS : (l + 1) * TERMS, :])
-            halo_l[0:EDGE, cols], halo_l[EDGE:, cols] = split(halo_f[c, l * EDGE : (l + 1) * EDGE, :])
-            cal_l[0:32, cols], cal_l[32:, cols] = split(cal_f[c, l * 32 : (l + 1) * 32, :])
+            att_l[c, 0:TERMS, cols], att_l[c, TERMS:, cols] = split(att_f[c, l * TERMS_STEP : l * TERMS_STEP + TERMS, :])
+            halo_l[c, 0:EDGE, cols], halo_l[c, EDGE:, cols] = split(halo_f[c, l * EDGE_STEP : l * EDGE_STEP + EDGE, :])
+            cal_l[c, 0:32, cols], cal_l[c, 32:, cols] = split(cal_f[c, l * CAL_STEP : l * CAL_STEP + 32, :])
 
             def label(f):
-                return turned_s[c, LOW * f + l : LOW * f + l + 1, :].astype(jnp.int32)
-
-            knot_hot[:, cols] = onehot(SEG, 0, label(6))
-            ccd_hot[:, cols] = onehot(SEG, 0, label(13))
-            halo_hot[:, cols] = onehot(16, SEG - 16, label(FIELDS + 6))
-    main = nt_dot(att_l[...], knot_hot[...])
+                return turned_s[c, LOW * f + l : LOW * f + l + 1, :]
+
+            knot_hot[c, :, cols] = label_hot(SEG, 0, label(6))
+            ccd_hot[c, :, cols] = label_hot(SEG, 0, label(13))
+            halo_hot[c, :, cols] = label_hot(16, SEG - 16, label(FIELDS + 6))
+        sums = (
+            nt_dot(att_l[c], knot_hot[c]),
+            nt_dot(halo_l[c], halo_hot[c]),
+            nt_dot(cal_l[c], ccd_hot[c]),
+        )
+        totals = sums if c == 0 else tuple(x + y for x, y in zip(totals, sums))
+    main, edge, cal = totals
     main = main[:TERMS] + main[TERMS:]
-    edge = nt_dot(halo_l[...], halo_hot[...])
     edge = edge[:EDGE] + edge[EDGE:]
     edge = jnp.concatenate([jnp.zeros((EDGE, LANES - 16), F32), edge], 1)
     total = main[: GROUP_ROWS[0]]
@@ -219,7 +231,6 @@
         if n < GROUP_ROWS[0]:
             group = jnp.concatenate([group, jnp.zeros((GROUP_ROWS[0] - n, SEG), F32)], 0)
         total = total + group
-    cal = nt_dot(cal_l[...], ccd_hot[...])
     cal = cal[:32] + cal[32:]
     for z in range(out.shape[0]):
         out[z, 0:48, :] = total
@@ -307,21 +318,21 @@
     )
     got, src_normal, src_rhs = lax.optimization_barrier((got, src_normal, src_rhs))
     chunks = tm_count * 8 // LANES
-    depth = chunks * LOW * LANES
+    depth = LOW * LANES
     sums = call(
         time_kernel,
         shape(z_count, 72, SEG),
         [
             pltpu.VMEM((chunks, LANES, LANES), F32),
-            pltpu.VMEM((chunks, LOW * TERMS, LANES), F32),
-            pltpu.VMEM((chunks, LOW * EDGE, LANES), F32),
-            pltpu.VMEM((chunks, LOW * 32, LANES), F32),
-            pltpu.VMEM((2 * TERMS, depth), BF16),
-            pltpu.VMEM((2 * EDGE, depth), BF16),
-            pltpu.VMEM((64, depth), BF16),
-            pltpu.VMEM((SEG, depth), BF16),
-            pltpu.VMEM((16, depth), BF16),
-            pltpu.VMEM((SEG, depth), BF16),
+            pltpu.VMEM((chunks, 8 * TERMS_STEP, LANES), F32),
+            pltpu.VMEM((chunks, 8 * EDGE_STEP, LANES), F32),
+            pltpu.VMEM((chunks, 8 * CAL_STEP, LANES), F32),
+            pltpu.VMEM((chunks, 2 * TERMS, depth), BF16),
+            pltpu.VMEM((chunks, 2 * EDGE, depth), BF16),
+            pltpu.VMEM((chunks, 64, depth), BF16),
+            pltpu.VMEM((chunks, SEG, depth), BF16),
+            pltpu.VMEM((chunks, 16, depth), BF16),
+            pltpu.VMEM((chunks, SEG, depth), BF16),
         ],
         24,
         1000000000,

time: 60.9 us -> 59.3 us (0.974)
  Pallas kernels: 8.54 us -> 6.85 us
    pallas_call x4, Pallas kernels: 8.54 us -> 6.85 us  [call(): pl.pallas_call(kernel, out_shape=out_shape, in_specs=[pl.BlockSpec(memory...]
where the time goes in v4:
time: 59.3 us; the launch traced here: 59 us
  blocking collectives  28.3 us (48%)
  starting transfers between devices  11.8 us (20%)
  waiting for transfers between devices  11.4 us (19%)
  Pallas kernels  6.85 us (12%)
  between operations  0.72 us (1%)
    all_to_all x1, blocking collectives, local(): parts = lax.all_to_all(sums, 'src', split_axis=0, concat_axis=0, tiled=True)  28.3 us
    all_to_all x1, starting transfers between devices, local(): got = lax.all_to_all(send, 'tm', split_axis=0, concat_axis=0, tiled=True)  11.8 us
    all_to_all x1, waiting for transfers between devices, local(): got = lax.all_to_all(send, 'tm', split_axis=0, concat_axis=0, tiled=True)  11.4 us
    pallas_call x4, Pallas kernels, call(): pl.pallas_call(kernel, out_shape=out_shape, in_specs=[pl.BlockSpec(memory...  6.85 us
  transfers between devices with their start and end apart: 1, of which 1 were waited for; matrix products, arithmetic and copies ran while one was open for 0% of the time, Pallas kernels for 3%

profile of v4, /device:TPU:1, one launch (start us, length us, event | category | flops | bytes accessed | tf_op | source)
XLA Modules:
  0.0 59.0 jit_solution(7431809427581746926)
XLA Ops:
  0.6 2.5 %shard_map.136 = f32[64,8,128]{2,1,0:T(8,128)} custom-call(f32[4,1536]{1,0:T(4,128)} %refs_0_.1, f32[1536]{0:T(1024)} %refs_1_.1, f32[6,1536]{1,0:T(8,128)} %refs_2_.1, f32[1536]{0:T(1024)} %resid.1, f32[1536]{0:T(1024)} %weight.1, s32[1536]{0:T(1024)} %refs_5_.1, s32[1536]{0:T(1024)} %refs_6_.1), custom_call_target="tpu_custom_call" | custom-call | flops 1000000000 | bytes 200000 | tf_op jit(solution)/shard_map/pallas_call | solution.py:267
  3.1 0.0 copy-start
  3.1 0.0 copy-start.1
  3.2 0.0 copy-start.2
  3.2 0.0 copy-start.3
  3.2 11.8 %all-to-all-start = ((f32[64,8,128]{2,1,0:T(8,128)}), f32[64,8,128]{2,1,0:T(8,128)S(1)}, u32[]{:S(2)}, u32[]{:S(2)}) async-start(f32[64,8,128]{2,1,0:T(8,128)} %shard_map.136), calls=%async_computation | async-start | bytes 524288 | tf_op jit(solution)/shard_map/all_to_all | solution.py:307
  15.0 0.0 copy-done
  15.0 0.0 copy-done.1
  15.0 0.0 copy-done.2
  15.0 0.0 copy-done.3
  15.0 1.8 %shard_map.137 = (f32[5,5,1024]{2,1,0:T(8,128)}, f32[5,1024]{1,0:T(8,128)}) custom-call(f32[5,1536]{1,0:T(8,128)S(1)} %copy-done, f32[1536]{0:T(1024)S(1)} %copy-done.1, f32[1536]{0:T(1024)S(1)} %copy-done.2, s32[1536]{0:T(1024)S(1)} %copy-done.3), custom_call_target="tpu_custom_call" | custom-call | flops 4000000000 | bytes 200000 | tf_op jit(solution)/shard_map/pallas_call | solution.py:267
  16.8 11.4 %all-to-all-done.got = f32[64,8,128]{2,1,0:T(8,128)S(1)} async-done(((f32[64,8,128]{2,1,0:T(8,128)}), f32[64,8,128]{2,1,0:T(8,128)S(1)}, u32[]{:S(2)}, u32[]{:S(2)}) %all-to-all-start) | async-done | bytes 262176 | tf_op jit(solution)/shard_map/all_to_all | solution.py:307
  28.1 1.9 %shard_map.138 = f32[8,72,256]{2,1,0:T(8,128)S(1)} custom-call(f32[64,8,128]{2,1,0:T(8,128)S(1)} %all-to-all-done.got), custom_call_target="tpu_custom_call" | custom-call | flops 1000000000 | bytes 200000 | tf_op jit(solution)/shard_map/pallas_call | solution.py:267
  30.0 28.3 %all_to_all.10.parts = f32[8,72,256]{2,1,0:T(8,128)S(1)} all-to-all(f32[8,72,256]{2,1,0:T(8,128)S(1)} %shard_map.138), channel_id=1, replica_groups=mesh['tm'=64,'src'=8] {'src'}, dimensions={0} | all-to-all | bytes 1179648 | tf_op jit(solution)/shard_map/all_to_all | solution.py:341
  58.2 0.7 %shard_map.139 = (f32[4,4,4,256]{3,2,1,0:T(4,128)}, f32[4,256]{1,0:T(4,128)}, f32[6,6,256]{2,1,0:T(8,128)}, f32[6,256]{1,0:T(8,128)}) custom-call(f32[8,72,256]{2,1,0:T(8,128)S(1)} %all_to_all.10.parts), custom_call_target="tpu_custom_call" | custom-call | flops 1000000 | bytes 200000 | tf_op jit(solution)/shard_map/pallas_call | solution.py:267
Async XLA Ops:
  3.1 11.8 %copy-start = (f32[5,1536]{1,0:T(8,128)S(1)}, f32[5,1536]{1,0:T(8,128)}, u32[]{:S(2)}) copy-start(f32[5,1536]{1,0:T(8,128)} %partials.1) | copy-start | bytes 92164
  3.1 11.8 %copy-start.1 = (f32[1536]{0:T(1024)S(1)}, f32[1536]{0:T(1024)}, u32[]{:S(2)}) copy-start(f32[1536]{0:T(1024)} %resid.1) | copy-start | bytes 18436
  3.2 11.8 %copy-start.2 = (f32[1536]{0:T(1024)S(1)}, f32[1536]{0:T(1024)}, u32[]{:S(2)}) copy-start(f32[1536]{0:T(1024)} %weight.1) | copy-start | bytes 18436
  3.2 11.8 %copy-start.3 = (s32[1536]{0:T(1024)S(1)}, s32[1536]{0:T(1024)}, u32[]{:S(2)}) copy-start(s32[1536]{0:T(1024)} %ids.1) | copy-start | bytes 18436
  3.2 24.9 %all-to-all-start = ((f32[64,8,128]{2,1,0:T(8,128)}), f32[64,8,128]{2,1,0:T(8,128)S(1)}, u32[]{:S(2)}, u32[]{:S(2)}) async-start(f32[64,8,128]{2,1,0:T(8,128)} %shard_map.136), calls=%async_computation | async-start | bytes 524288 | tf_op jit(solution)/shard_map/all_to_all | solution.py:307

commit v5 on v4

--- a/solution.py
+++ b/solution.py
@@ -11,10 +11,11 @@
 F32 = jnp.float32
 BF16 = jnp.bfloat16
 
-LOW = 6
+LOW = 8
+HIGH = 6
 FIELDS = 14
-HALO_FIELDS = 7
-HALO_LANE = LOW * FIELDS
+SPILL = [(0, 0), (1, 0), (2, 0), (0, 1), (1, 1), (0, 2)]
+SPILL_LANE = LOW * FIELDS
 ATT_PAIRS = [(c, e) for c in range(4) for e in range(c, 4)]
 CAL_PAIRS = [(p, q) for p in range(6) for q in range(p, 6)]
 SRC_PAIRS = [(p, q) for p in range(5) for q in range(p, 5)]
@@ -22,8 +23,7 @@
 GROUP_START = [0, 48, 88, 112]
 TERMS = 128
 PACK_MIB = 56
-EDGE = TERMS - GROUP_START[1]
-TERMS_STEP, EDGE_STEP, CAL_STEP = TERMS + 1, EDGE + 1, 32 + 1
+TERMS_STEP, CAL_STEP = TERMS + 1, 32 + 1
 
 
 def nt_dot(left, right):
@@ -50,9 +50,9 @@
 
 def pack_kernel(*refs):
     count = 7
-    hot_s, val_s = refs[count + 1 : count + 3]
     out = refs[count]
-    held = refs[count + 3 : -1]
+    hot_s, val_s, spill_s, tile_s = refs[count + 1 : count + 5]
+    held = refs[count + 5 : -1]
     copies = [
         pltpu.make_async_copy(refs[i], held[i], refs[-1].at[i]) for i in range(count)
     ]
@@ -84,48 +84,76 @@
             )
         carry = carry + counts[:, chunk:]
     rank = jnp.concatenate(ranks, 1).astype(jnp.int32)
-    high = (rank * 43) >> 8
-    low = rank - LOW * high
+    high = rank >> 3
+    low = rank & 7
 
     for i in (0, 1, 2, 3, 4, 6):
         copies[i].wait()
     scale = jnp.sqrt(weight[...].reshape(1, obs))
     geoms = geom[...] * scale
     cals = cal[...] * scale
-    fields = [geoms[c : c + 1] for c in range(4)]
-    fields += [frac[...].reshape(1, obs), resid[...].reshape(1, obs) * scale]
-    fields += [(knots - SEG * seg).astype(F32)]
+    place = knots - SEG * seg
+    frac_row = frac[...].reshape(1, obs)
+    geom_rows = [geoms[c : c + 1] for c in range(4)]
+    resid_row = resid[...].reshape(1, obs) * scale
+    fields = geom_rows + [frac_row, resid_row, place.astype(F32)]
     fields += [cals[p : p + 1] for p in range(6)]
     fields += [ccd[...].reshape(1, obs).astype(F32)]
+
+    basis = spline_basis(frac_row)
+    spill = []
+    for j in range(3):
+        value = jnp.zeros_like(frac_row)
+        for a in range(j + 1, 4):
+            value = jnp.where(place == SEG + j - a, basis[a], value)
+        spill.append(value)
+    left = [geom_rows[c] for c, _ in ATT_PAIRS] + [resid_row] * 4
+    right = [geom_rows[e] for _, e in ATT_PAIRS] + geom_rows
+    zero = jnp.zeros((1, obs), F32)
+    both = [
+        jnp.concatenate(left[at : at + 8] + [zero] * max(0, at + 8 - 14), 0)
+        * jnp.concatenate(right[at : at + 8] + [zero] * max(0, at + 8 - 14), 0)
+        for at in (0, 8)
+    ]
+    sub = lax.broadcasted_iota(jnp.int32, (8, obs), 0)
+    for s, (j, d) in enumerate(SPILL):
+        pair = spill[j] * spill[j + d]
+        other = spill[j] if d == 0 else zero
+        terms = [both[0] * pair, both[1] * jnp.where(sub < 2, pair, other)]
+        top, rest = split(jnp.concatenate(terms, 0))
+        spill_s[16 * s : 16 * s + 16, :] = top
+        spill_s[LANES + 16 * s : LANES + 16 * s + 16, :] = rest
+    for at in (16 * HIGH, LANES + 16 * HIGH):
+        spill_s[at : at + LANES - 16 * HIGH, :] = jnp.zeros((LANES - 16 * HIGH, obs), BF16)
+
     fields = jnp.concatenate(fields, 0)
     rounded = fields.astype(BF16).astype(F32)
-    parts = (rounded, fields - rounded)
-    sub = lax.broadcasted_iota(jnp.int32, (8, obs), 0)
-    masks = [(sub + 8 * j) % LOW == low for j in range(3)]
-    for i, part in enumerate(parts):
-        tiles = []
-        for j in range(LANES // 8):
-            first, last = 8 * j // LOW, (8 * j + 7) // LOW
-            if first >= FIELDS:
-                tiles.append(jnp.zeros((8, obs), F32))
-                continue
-            value = jnp.broadcast_to(part[first : first + 1], (8, obs))
-            for f in range(first + 1, last + 1):
-                row = part[f : f + 1] if f < FIELDS else 0.0
-                value = jnp.where(sub < LOW * f - 8 * j, value, row)
-            tiles.append(jnp.where(masks[j % 3], value, 0.0))
-        for j in range(0, LANES // 8, 2):
-            at = i * LANES + 8 * j
-            val_s[at : at + 16, :] = jnp.concatenate(tiles[j : j + 2], 0).astype(BF16)
-    code = seg * 8 + high
-    for j in range(0, 8 * segs, 64):
+    low_is = sub == low
+    for i, part in enumerate((rounded, fields - rounded)):
+        for f in range(0, FIELDS, 2):
+            pair = [jnp.where(low_is, part[f + n : f + n + 1], 0.0) for n in range(2)]
+            at = i * LANES + LOW * f
+            val_s[at : at + 16, :] = jnp.concatenate(pair, 0).astype(BF16)
+        val_s[i * LANES + SPILL_LANE : (i + 1) * LANES, :] = jnp.zeros((16, obs), BF16)
+    code = (high >> 1) * (2 * segs) + 2 * seg + (high & 1)
+    for j in range(0, HIGH * segs, 64):
         hot_s[j : j + 64, :] = label_hot(64, 0, (code - j).astype(F32))
     main = nt_dot(hot_s[...], val_s[...])
     main = main[:, :LANES] + main[:, LANES:]
-    lane = lax.broadcasted_iota(jnp.int32, (8 * segs, LANES), 1)
-    shifted = jnp.concatenate([jnp.zeros((8, LANES), F32), main[:-8]], 0)
-    shifted = pltpu.roll(shifted, HALO_LANE, 1)
-    out[...] = jnp.where(lane < HALO_LANE, main, shifted).reshape(segs, 8, LANES)
+    row = lax.broadcasted_iota(jnp.int32, (2 * segs, obs), 0) >> 1
+    sums = nt_dot(jnp.where(row == seg + 1, 1.0, 0.0).astype(BF16), spill_s[...])
+    sums = sums[:, :LANES] + sums[:, LANES:]
+    lane = lax.broadcasted_iota(jnp.int32, (2 * segs, LANES), 1)
+    even = lax.broadcasted_iota(jnp.int32, (2 * segs, LANES), 0) & 1 == 0
+    for m in range(HIGH // 2):
+        edge = jnp.where(
+            even,
+            pltpu.roll(sums, SPILL_LANE - 32 * m, 1),
+            pltpu.roll(sums, SPILL_LANE - 32 * m - 16, 1),
+        )
+        tile_s[m] = jnp.where(lane < SPILL_LANE, main[2 * segs * m : 2 * segs * (m + 1)], edge)
+        for t in range(segs):
+            out[t, :, m * LANES : (m + 1) * LANES] = tile_s[m, 2 * t : 2 * t + 2, :]
 
 
 def source_kernel(partials, resid, weight, ids, normal, rhs, left_s):
@@ -154,22 +182,25 @@
         rhs[:, j : j + step] = sums[len(SRC_PAIRS) : len(SRC_PAIRS) + count]
 
 
-def att_terms(rows, first):
-    geoms = rows[:4]
-    frac, resid = rows[4], rows[5]
+def spline_basis(frac):
     remain = 1.0 - frac
     square = frac * frac
     cubic = square * frac
-    basis = [
+    return [
         remain * remain * remain * (1.0 / 6.0),
         (3.0 * cubic - 6.0 * square + 4.0) * (1.0 / 6.0),
         (-3.0 * cubic + 3.0 * square + 3.0 * frac + 1.0) * (1.0 / 6.0),
         cubic * (1.0 / 6.0),
     ]
+
+
+def att_terms(rows):
+    geoms, frac, resid = rows[:4], rows[4], rows[5]
+    basis = spline_basis(frac)
     pairs = [geoms[c] * geoms[e] for c, e in ATT_PAIRS]
     weighted = [geoms[c] * resid for c in range(4)]
     terms = []
-    for a in range(first, 4):
+    for a in range(4):
         place = GROUP_START[a]
         for c in range(4):
             terms.append((place + c, basis[a] * weighted[c]))
@@ -184,12 +215,19 @@
     return terms
 
 
-def time_kernel(got, out, turned_s, att_f, halo_f, cal_f, att_l, halo_l, cal_l, knot_hot, halo_hot, ccd_hot):
-    chunks = got.shape[0] * 8 // LANES
-    for c in range(chunks):
-        turned_s[c] = got[c * 16 : (c + 1) * 16].reshape(LANES, LANES).T
-        rows = [turned_s[c, LOW * f : LOW * f + LOW, :] for f in range(FIELDS + HALO_FIELDS)]
-        for t, value in att_terms(rows, 0):
+def time_kernel(got, out, tile_s, turned_s, att_f, cal_f, att_l, cal_l, knot_hot, ccd_hot, edge_s, sum_s):
+    segs = got.shape[0]
+    columns = []
+    parity = lax.broadcasted_iota(jnp.int32, (16, LANES), 1) & 1
+    for c in range(HIGH // 2):
+        for t in range(segs):
+            tile_s[c, 2 * t : 2 * t + 2, :] = got[t, :, c * LANES : (c + 1) * LANES]
+        turned_s[c] = tile_s[c].T
+        edge = turned_s[c, SPILL_LANE:, :]
+        for r in range(2):
+            columns.append(jnp.sum(jnp.where(parity == r, edge, 0.0), 1, keepdims=True))
+        rows = [turned_s[c, LOW * f : LOW * f + LOW, :] for f in range(FIELDS)]
+        for t, value in att_terms(rows):
             att_f[c, pl.ds(t, LOW, stride=TERMS_STEP), :] = value
         cals = rows[7:13]
         terms = [cals[p] * cals[q] for p, q in CAL_PAIRS]
@@ -197,52 +235,65 @@
         terms += [jnp.zeros((LOW, LANES), F32)] * (32 - len(terms))
         for t, value in enumerate(terms):
             cal_f[c, pl.ds(t, LOW, stride=CAL_STEP), :] = value
-        for t, value in att_terms(rows[FIELDS:], 1):
-            halo_f[c, pl.ds(t - GROUP_START[1], LOW, stride=EDGE_STEP), :] = value
         for l in range(LOW):
-            at = l * LANES
-            cols = slice(at, at + LANES)
-            att_l[c, 0:TERMS, cols], att_l[c, TERMS:, cols] = split(att_f[c, l * TERMS_STEP : l * TERMS_STEP + TERMS, :])
-            halo_l[c, 0:EDGE, cols], halo_l[c, EDGE:, cols] = split(halo_f[c, l * EDGE_STEP : l * EDGE_STEP + EDGE, :])
-            cal_l[c, 0:32, cols], cal_l[c, 32:, cols] = split(cal_f[c, l * CAL_STEP : l * CAL_STEP + 32, :])
-
-            def label(f):
-                return turned_s[c, LOW * f + l : LOW * f + l + 1, :]
-
-            knot_hot[c, :, cols] = label_hot(SEG, 0, label(6))
-            ccd_hot[c, :, cols] = label_hot(SEG, 0, label(13))
-            halo_hot[c, :, cols] = label_hot(16, SEG - 16, label(FIELDS + 6))
-        sums = (
-            nt_dot(att_l[c], knot_hot[c]),
-            nt_dot(halo_l[c], halo_hot[c]),
-            nt_dot(cal_l[c], ccd_hot[c]),
-        )
+            cols = slice(l * LANES, (l + 1) * LANES)
+            att_l[c, 0:TERMS, cols], att_l[c, TERMS:, cols] = split(
+                att_f[c, l * TERMS_STEP : l * TERMS_STEP + TERMS, :]
+            )
+            cal_l[c, 0:32, cols], cal_l[c, 32:, cols] = split(
+                cal_f[c, l * CAL_STEP : l * CAL_STEP + 32, :]
+            )
+            for hot, f in ((knot_hot, 6), (ccd_hot, 13)):
+                at = LOW * f + l
+                hot[c, :, cols] = label_hot(SEG, 0, turned_s[c, at : at + 1, :])
+        sums = (nt_dot(att_l[c], knot_hot[c]), nt_dot(cal_l[c], ccd_hot[c]))
         totals = sums if c == 0 else tuple(x + y for x, y in zip(totals, sums))
-    main, edge, cal = totals
+    main, cal = totals
     main = main[:TERMS] + main[TERMS:]
-    edge = edge[:EDGE] + edge[EDGE:]
-    edge = jnp.concatenate([jnp.zeros((EDGE, LANES - 16), F32), edge], 1)
+    cal = cal[:32] + cal[32:]
+    lane = lax.broadcasted_iota(jnp.int32, (16, LANES), 1)
+    edge_s[...] = jnp.zeros(edge_s.shape, F32)
+    for d in range(3):
+        block = jnp.zeros((16, LANES), F32)
+        for s, (j, gap) in enumerate(SPILL):
+            if gap == d:
+                block = jnp.where(lane == j, columns[s], block)
+        edge_s[4 + 10 * d : 14 + 10 * d, :] = block[0:10]
+        if d == 0:
+            edge_s[0:4, :] = block[10:14]
     total = main[: GROUP_ROWS[0]]
     for a in range(1, 4):
         n = GROUP_ROWS[a]
-        at = GROUP_START[a]
-        group = jnp.concatenate([edge[at - GROUP_START[1] :][:n], main[at : at + n]], 1)
-        group = pltpu.roll(group, a, 1)[:, LANES:]
+        group = pltpu.roll(main[GROUP_START[a] : GROUP_START[a] + n], a, 1)
+        group = jnp.where(lax.broadcasted_iota(jnp.int32, (n, SEG), 1) < a, 0.0, group)
         if n < GROUP_ROWS[0]:
             group = jnp.concatenate([group, jnp.zeros((GROUP_ROWS[0] - n, SEG), F32)], 0)
         total = total + group
-    cal = cal[:32] + cal[32:]
+    for h in range(2):
+        cols = slice(h * LANES, (h + 1) * LANES)
+        sum_s[72 * h : 72 * h + 48, :] = total[:, cols] + edge_s[...] if h == 0 else total[:, cols]
+        sum_s[72 * h + 48 : 72 * h + 72, :] = cal[0:24, cols]
+        sum_s[72 * h + 44 : 72 * h + 47, :] = cal[24:27, cols]
     for z in range(out.shape[0]):
-        out[z, 0:48, :] = total
-        out[z, 48:72, :] = cal[0:24]
-        out[z, 44:47, :] = cal[24:27]
-
-
-def final_kernel(parts, att_normal, att_rhs, cal_normal, cal_rhs, sum_s):
+        for j in range(9):
+            at = 18 * z + 2 * j
+            out[z, :, j * LANES : (j + 1) * LANES] = sum_s[at : at + 2, :]
+
+
+def middle_kernel(parts, out):
     total = parts[0]
     for z in range(1, parts.shape[0]):
         total = total + parts[z]
-    sum_s[...] = total
+    for z in range(out.shape[0]):
+        out[z] = total
+
+
+def final_kernel(parts, att_normal, att_rhs, cal_normal, cal_rhs, sum_s):
+    for z in range(parts.shape[0]):
+        for j in range(9):
+            half, at = divmod(18 * z + 2 * j, 72)
+            cols = slice(half * LANES, (half + 1) * LANES)
+            sum_s[at : at + 2, cols] = parts[z, :, j * LANES : (j + 1) * LANES]
     att_rhs[...] = sum_s[0:4, :]
     for d in range(4):
         for q, (c, e) in enumerate(ATT_PAIRS):
@@ -295,8 +346,13 @@
     rows = (att_geom, spline_frac, cal_partials, residual, weight, knot_ids, ccd_ids)
     send = call(
         pack_kernel,
-        shape(tm_count, 8, LANES),
-        [pltpu.VMEM((8 * tm_count, obs), BF16), pltpu.VMEM((2 * LANES, obs), BF16)]
+        shape(tm_count, 2, HIGH // 2 * LANES),
+        [
+            pltpu.VMEM((HIGH * tm_count, obs), BF16),
+            pltpu.VMEM((2 * LANES, obs), BF16),
+            pltpu.VMEM((2 * LANES, obs), BF16),
+            pltpu.VMEM((HIGH // 2, 2 * tm_count, LANES), F32),
+        ]
         + [pltpu.VMEM(x.shape, x.dtype) for x in rows]
         + [pltpu.SemaphoreType.DMA((len(rows),))],
         PACK_MIB,
@@ -317,28 +373,30 @@
         source_ids,
     )
     got, src_normal, src_rhs = lax.optimization_barrier((got, src_normal, src_rhs))
-    chunks = tm_count * 8 // LANES
+    chunks = HIGH // 2
     depth = LOW * LANES
     sums = call(
         time_kernel,
-        shape(z_count, 72, SEG),
+        shape(z_count, 2, 9 * LANES),
         [
+            pltpu.VMEM((chunks, 2 * tm_count, LANES), F32),
             pltpu.VMEM((chunks, LANES, LANES), F32),
-            pltpu.VMEM((chunks, 8 * TERMS_STEP, LANES), F32),
-            pltpu.VMEM((chunks, 8 * EDGE_STEP, LANES), F32),
-            pltpu.VMEM((chunks, 8 * CAL_STEP, LANES), F32),
+            pltpu.VMEM((chunks, LOW * TERMS_STEP, LANES), F32),
+            pltpu.VMEM((chunks, LOW * CAL_STEP, LANES), F32),
             pltpu.VMEM((chunks, 2 * TERMS, depth), BF16),
-            pltpu.VMEM((chunks, 2 * EDGE, depth), BF16),
             pltpu.VMEM((chunks, 64, depth), BF16),
             pltpu.VMEM((chunks, SEG, depth), BF16),
-            pltpu.VMEM((chunks, 16, depth), BF16),
             pltpu.VMEM((chunks, SEG, depth), BF16),
+            pltpu.VMEM((48, LANES), F32),
+            pltpu.VMEM((144, LANES), F32),
         ],
         24,
         1000000000,
         got,
     )
     parts = lax.all_to_all(sums, "src", split_axis=0, concat_axis=0, tiled=True)
+    parts = call(middle_kernel, shape(z_count, 2, 9 * LANES), [], 8, 1000000, parts)
+    parts = lax.all_to_all(parts, "src", split_axis=0, concat_axis=0, tiled=True)
     att_normal, att_rhs, cal_normal, cal_rhs = call(
         final_kernel,
         (shape(4, 4, 4, SEG), shape(4, SEG), shape(6, 6, SEG), shape(6, SEG)),

time: 59.3 us -> 57.7 us (0.973); the launches traced: 59 us -> 56.6 us
  blocking collectives: 28.3 us -> 26.8 us
  waiting for transfers between devices: 11.4 us -> 10.2 us
    all_to_all x1, blocking collectives: 28.3 us -> 17 us  [local(): parts = lax.all_to_all(sums, 'src', split_axis=0, concat_axis=0, tiled=True)]
    all_to_all x0 -> x1, blocking collectives: none -> 9.8 us  [local(): lax.all_to_all(parts, 'src', split_axis=0, concat_axis=0, tiled=True)]
    all_to_all x1, waiting for transfers between devices: 11.4 us -> 10.2 us  [local(): got = lax.all_to_all(send, 'tm', split_axis=0, concat_axis=0, tiled=True)]
    pallas_call x4 -> x5, Pallas kernels: 6.85 us -> 7.01 us  [call(): pl.pallas_call(kernel, out_shape=out_shape, in_specs=[pl.BlockSpec(memory...]
where the time goes in v5:
time: 57.7 us; the launch traced here: 56.6 us
  blocking collectives  26.8 us (46%)
  starting transfers between devices  11.8 us (20%)
  waiting for transfers between devices  10.2 us (18%)
  Pallas kernels  7.01 us (12%)
  between operations  0.72 us (1%)
    all_to_all x1, blocking collectives, local(): parts = lax.all_to_all(sums, 'src', split_axis=0, concat_axis=0, tiled=True)  17 us
    all_to_all x1, starting transfers between devices, local(): got = lax.all_to_all(send, 'tm', split_axis=0, concat_axis=0, tiled=True)  11.8 us
    all_to_all x1, waiting for transfers between devices, local(): got = lax.all_to_all(send, 'tm', split_axis=0, concat_axis=0, tiled=True)  10.2 us
    all_to_all x1, blocking collectives, local(): lax.all_to_all(parts, 'src', split_axis=0, concat_axis=0, tiled=True)  9.8 us
    pallas_call x5, Pallas kernels, call(): pl.pallas_call(kernel, out_shape=out_shape, in_specs=[pl.BlockSpec(memory...  7.01 us
  transfers between devices with their start and end apart: 1, of which 1 were waited for; matrix products, arithmetic and copies ran while one was open for 0% of the time, Pallas kernels for 3%

profile of v5, /device:TPU:1, one launch (start us, length us, event | category | flops | bytes accessed | tf_op | source)
XLA Modules:
  0.0 56.6 jit_solution(672392236019286196)
XLA Ops:
  0.6 2.6 %shard_map.136 = f32[64,2,384]{2,1,0:T(2,128)} custom-call(f32[4,1536]{1,0:T(4,128)} %refs_0_.1, f32[1536]{0:T(1024)} %refs_1_.1, f32[6,1536]{1,0:T(8,128)} %refs_2_.1, f32[1536]{0:T(1024)} %resid.1, f32[1536]{0:T(1024)} %weight.1, s32[1536]{0:T(1024)} %refs_5_.1, s32[1536]{0:T(1024)} %refs_6_.1), custom_call_target="tpu_custom_call" | custom-call | flops 1000000000 | bytes 200000 | tf_op jit(solution)/shard_map/pallas_call | solution.py:318
  3.3 0.0 copy-start
  3.3 0.0 copy-start.1
  3.3 0.0 copy-start.2
  3.3 0.0 copy-start.3
  3.3 11.8 %all-to-all-start = ((f32[64,2,384]{2,1,0:T(2,128)}), f32[64,2,384]{2,1,0:T(2,128)S(1)}, u32[]{:S(2)}, u32[]{:S(2)}) async-start(f32[64,2,384]{2,1,0:T(2,128)} %shard_map.136), calls=%async_computation | async-start | bytes 393216 | tf_op jit(solution)/shard_map/all_to_all | solution.py:363
  15.1 0.0 copy-done
  15.1 0.0 copy-done.1
  15.1 0.0 copy-done.2
  15.1 0.0 copy-done.3
  15.1 1.8 %shard_map.137 = (f32[5,5,1024]{2,1,0:T(8,128)}, f32[5,1024]{1,0:T(8,128)}) custom-call(f32[5,1536]{1,0:T(8,128)S(1)} %copy-done, f32[1536]{0:T(1024)S(1)} %copy-done.1, f32[1536]{0:T(1024)S(1)} %copy-done.2, s32[1536]{0:T(1024)S(1)} %copy-done.3), custom_call_target="tpu_custom_call" | custom-call | flops 4000000000 | bytes 200000 | tf_op jit(solution)/shard_map/pallas_call | solution.py:318
  16.9 10.2 %all-to-all-done.got = f32[64,2,384]{2,1,0:T(2,128)S(1)} async-done(((f32[64,2,384]{2,1,0:T(2,128)}), f32[64,2,384]{2,1,0:T(2,128)S(1)}, u32[]{:S(2)}, u32[]{:S(2)}) %all-to-all-start) | async-done | bytes 196640 | tf_op jit(solution)/shard_map/all_to_all | solution.py:363
  27.1 1.9 %shard_map.138 = f32[8,2,1152]{2,1,0:T(2,128)S(1)} custom-call(f32[64,2,384]{2,1,0:T(2,128)S(1)} %all-to-all-done.got), custom_call_target="tpu_custom_call" | custom-call | flops 1000000000 | bytes 200000 | tf_op jit(solution)/shard_map/pallas_call | solution.py:318
  29.0 17.0 %all_to_all.15.parts = f32[8,2,1152]{2,1,0:T(2,128)S(1)} all-to-all(f32[8,2,1152]{2,1,0:T(2,128)S(1)} %shard_map.138), channel_id=1, replica_groups=mesh['tm'=64,'src'=8] {'src'}, dimensions={0} | all-to-all | bytes 147456 | tf_op jit(solution)/shard_map/all_to_all | solution.py:397
  46.1 9.8 %all_to_all.16.parts = f32[8,2,1152]{2,1,0:T(2,128)S(1)} all-to-all(f32[8,2,1152]{2,1,0:T(2,128)S(1)} %shard_map.139), channel_id=1, replica_groups=mesh['tm'=64,'src'=8] {'src'}, dimensions={0} | all-to-all | bytes 147456 | tf_op jit(solution)/shard_map/all_to_all | solution.py:399
  55.9 0.7 %shard_map.140 = (f32[4,4,4,256]{3,2,1,0:T(4,128)}, f32[4,256]{1,0:T(4,128)}, f32[6,6,256]{2,1,0:T(8,128)}, f32[6,256]{1,0:T(8,128)}) custom-call(f32[8,2,1152]{2,1,0:T(2,128)S(1)} %all_to_all.16.parts), custom_call_target="tpu_custom_call" | custom-call | flops 1000000 | bytes 200000 | tf_op jit(solution)/shard_map/pallas_call | solution.py:318
  (1 shorter events, 0.0 us)
Async XLA Ops:
  3.3 11.8 %copy-start = (f32[5,1536]{1,0:T(8,128)S(1)}, f32[5,1536]{1,0:T(8,128)}, u32[]{:S(2)}) copy-start(f32[5,1536]{1,0:T(8,128)} %partials.1) | copy-start | bytes 92164
  3.3 11.8 %copy-start.1 = (f32[1536]{0:T(1024)S(1)}, f32[1536]{0:T(1024)}, u32[]{:S(2)}) copy-start(f32[1536]{0:T(1024)} %resid.1) | copy-start | bytes 18436
  3.3 11.8 %copy-start.2 = (f32[1536]{0:T(1024)S(1)}, f32[1536]{0:T(1024)}, u32[]{:S(2)}) copy-start(f32[1536]{0:T(1024)} %weight.1) | copy-start | bytes 18436
  3.3 11.8 %copy-start.3 = (s32[1536]{0:T(1024)S(1)}, s32[1536]{0:T(1024)}, u32[]{:S(2)}) copy-start(s32[1536]{0:T(1024)} %ids.1) | copy-start | bytes 18436
  3.3 23.8 %all-to-all-start = ((f32[64,2,384]{2,1,0:T(2,128)}), f32[64,2,384]{2,1,0:T(2,128)S(1)}, u32[]{:S(2)}, u32[]{:S(2)}) async-start(f32[64,2,384]{2,1,0:T(2,128)} %shard_map.136), calls=%async_computation | async-start | bytes 393216 | tf_op jit(solution)/shard_map/all_to_all | solution.py:363

commit v6 on v5

--- a/solution.py
+++ b/solution.py
@@ -215,7 +215,7 @@
     return terms
 
 
-def time_kernel(got, out, tile_s, turned_s, att_f, cal_f, att_l, cal_l, knot_hot, ccd_hot, edge_s, sum_s):
+def time_kernel(got, out, tile_s, turned_s, att_f, cal_f, att_l, cal_l, knot_hot, ccd_hot, edge_s):
     segs = got.shape[0]
     columns = []
     parity = lax.broadcasted_iota(jnp.int32, (16, LANES), 1) & 1
@@ -269,15 +269,11 @@
         if n < GROUP_ROWS[0]:
             group = jnp.concatenate([group, jnp.zeros((GROUP_ROWS[0] - n, SEG), F32)], 0)
         total = total + group
-    for h in range(2):
-        cols = slice(h * LANES, (h + 1) * LANES)
-        sum_s[72 * h : 72 * h + 48, :] = total[:, cols] + edge_s[...] if h == 0 else total[:, cols]
-        sum_s[72 * h + 48 : 72 * h + 72, :] = cal[0:24, cols]
-        sum_s[72 * h + 44 : 72 * h + 47, :] = cal[24:27, cols]
     for z in range(out.shape[0]):
-        for j in range(9):
-            at = 18 * z + 2 * j
-            out[z, :, j * LANES : (j + 1) * LANES] = sum_s[at : at + 2, :]
+        out[z, 0:48, 0:LANES] = total[:, :LANES] + edge_s[...]
+        out[z, 0:48, LANES:] = total[:, LANES:]
+        out[z, 48:72, :] = cal[0:24]
+        out[z, 44:47, :] = cal[24:27]
 
 
 def middle_kernel(parts, out):
@@ -289,11 +285,10 @@
 
 
 def final_kernel(parts, att_normal, att_rhs, cal_normal, cal_rhs, sum_s):
-    for z in range(parts.shape[0]):
-        for j in range(9):
-            half, at = divmod(18 * z + 2 * j, 72)
-            cols = slice(half * LANES, (half + 1) * LANES)
-            sum_s[at : at + 2, cols] = parts[z, :, j * LANES : (j + 1) * LANES]
+    total = parts[0]
+    for z in range(1, parts.shape[0]):
+        total = total + parts[z]
+    sum_s[...] = total
     att_rhs[...] = sum_s[0:4, :]
     for d in range(4):
         for q, (c, e) in enumerate(ATT_PAIRS):
@@ -312,6 +307,12 @@
             cal_normal[q, p : p + 1, :] = cal_row(t)
     for p in range(6):
         cal_rhs[p : p + 1, :] = cal_row(21 + p)
+
+
+def exchange(blocks, groups):
+    return lax.all_to_all(
+        blocks, "src", split_axis=0, concat_axis=0, tiled=True, axis_index_groups=groups
+    )
 
 
 def call(kernel, out_shape, scratch, vmem_mib, cost, *args, space=pltpu.VMEM):
@@ -377,7 +378,7 @@
     depth = LOW * LANES
     sums = call(
         time_kernel,
-        shape(z_count, 2, 9 * LANES),
+        shape(2, 72, SEG),
         [
             pltpu.VMEM((chunks, 2 * tm_count, LANES), F32),
             pltpu.VMEM((chunks, LANES, LANES), F32),
@@ -388,15 +389,16 @@
             pltpu.VMEM((chunks, SEG, depth), BF16),
             pltpu.VMEM((chunks, SEG, depth), BF16),
             pltpu.VMEM((48, LANES), F32),
-            pltpu.VMEM((144, LANES), F32),
         ],
         24,
         1000000000,
         got,
     )
-    parts = lax.all_to_all(sums, "src", split_axis=0, concat_axis=0, tiled=True)
-    parts = call(middle_kernel, shape(z_count, 2, 9 * LANES), [], 8, 1000000, parts)
-    parts = lax.all_to_all(parts, "src", split_axis=0, concat_axis=0, tiled=True)
+    pairs = [[2 * g, 2 * g + 1] for g in range(z_count // 2)]
+    ranks = [[2 * g + i for g in range(z_count // 2)] for i in range(2)]
+    parts = exchange(sums, pairs)
+    parts = call(middle_kernel, shape(z_count // 2, 72, SEG), [], 8, 1000000, parts)
+    parts = exchange(parts, ranks)
     att_normal, att_rhs, cal_normal, cal_rhs = call(
         final_kernel,
         (shape(4, 4, 4, SEG), shape(4, SEG), shape(6, 6, SEG), shape(6, SEG)),

time: 57.7 us -> 56.4 us (0.977)
  the two profiles are of different devices: /device:TPU:1 before, /device:TPU:8 now
where the time goes in v6:
time: 56.4 us; the launch traced here: 56.1 us
  blocking collectives  28.1 us (50%)
  starting transfers between devices  10.7 us (19%)
  waiting for transfers between devices  9.52 us (17%)
  Pallas kernels  6.98 us (12%)
  between operations  0.73 us (1%)
    all_to_all x2, blocking collectives, exchange(): lax.all_to_all(blocks, 'src', split_axis=0, concat_axis=0, tiled=True, ax...  28.1 us
    all_to_all x1, starting transfers between devices, local(): got = lax.all_to_all(send, 'tm', split_axis=0, concat_axis=0, tiled=True)  10.7 us
    all_to_all x1, waiting for transfers between devices, local(): got = lax.all_to_all(send, 'tm', split_axis=0, concat_axis=0, tiled=True)  9.52 us
    pallas_call x5, Pallas kernels, call(): pl.pallas_call(kernel, out_shape=out_shape, in_specs=[pl.BlockSpec(memory...  6.98 us
  transfers between devices with their start and end apart: 1, of which 1 were waited for; matrix products, arithmetic and copies ran while one was open for 0% of the time, Pallas kernels for 3%

profile of v6, /device:TPU:8, one launch (start us, length us, event | category | flops | bytes accessed | tf_op | source)
XLA Modules:
  0.0 56.1 jit_solution(8861389287346044743)
XLA Ops:
  0.6 2.6 %shard_map.136 = f32[64,2,384]{2,1,0:T(2,128)} custom-call(f32[4,1536]{1,0:T(4,128)} %refs_0_.1, f32[1536]{0:T(1024)} %refs_1_.1, f32[6,1536]{1,0:T(8,128)} %refs_2_.1, f32[1536]{0:T(1024)} %resid.1, f32[1536]{0:T(1024)} %weight.1, s32[1536]{0:T(1024)} %refs_5_.1, s32[1536]{0:T(1024)} %refs_6_.1), custom_call_target="tpu_custom_call" | custom-call | flops 1000000000 | bytes 200000 | tf_op jit(solution)/shard_map/pallas_call | solution.py:319
  3.3 0.0 copy-start
  3.3 0.0 copy-start.1
  3.3 0.0 copy-start.2
  3.3 0.0 copy-start.3
  3.3 10.7 %all-to-all-start = ((f32[64,2,384]{2,1,0:T(2,128)}), f32[64,2,384]{2,1,0:T(2,128)S(1)}, u32[]{:S(2)}, u32[]{:S(2)}) async-start(f32[64,2,384]{2,1,0:T(2,128)} %shard_map.136), calls=%async_computation | async-start | bytes 393216 | tf_op jit(solution)/shard_map/all_to_all | solution.py:364
  14.0 0.0 copy-done
  14.1 0.0 copy-done.1
  14.1 0.0 copy-done.2
  14.1 0.0 copy-done.3
  14.1 1.8 %shard_map.137 = (f32[5,5,1024]{2,1,0:T(8,128)}, f32[5,1024]{1,0:T(8,128)}) custom-call(f32[5,1536]{1,0:T(8,128)S(1)} %copy-done, f32[1536]{0:T(1024)S(1)} %copy-done.1, f32[1536]{0:T(1024)S(1)} %copy-done.2, s32[1536]{0:T(1024)S(1)} %copy-done.3), custom_call_target="tpu_custom_call" | custom-call | flops 4000000000 | bytes 200000 | tf_op jit(solution)/shard_map/pallas_call | solution.py:319
  15.8 9.5 %all-to-all-done.got = f32[64,2,384]{2,1,0:T(2,128)S(1)} async-done(((f32[64,2,384]{2,1,0:T(2,128)}), f32[64,2,384]{2,1,0:T(2,128)S(1)}, u32[]{:S(2)}, u32[]{:S(2)}) %all-to-all-start) | async-done | bytes 196640 | tf_op jit(solution)/shard_map/all_to_all | solution.py:364
  25.4 1.9 %shard_map.138 = f32[2,72,256]{2,1,0:T(8,128)S(1)} custom-call(f32[64,2,384]{2,1,0:T(2,128)S(1)} %all-to-all-done.got), custom_call_target="tpu_custom_call" | custom-call | flops 1000000000 | bytes 200000 | tf_op jit(solution)/shard_map/pallas_call | solution.py:319
  27.2 8.0 %all_to_all.15.parts = f32[2,72,256]{2,1,0:T(8,128)S(1)} all-to-all(f32[2,72,256]{2,1,0:T(8,128)S(1)} %shard_map.138), channel_id=1, replica_groups={{0,1},{2,3},{4,5},{6,7},{8,9},{10,11},{12,13},{14,15},{16,17},{18,19},{..., dimensions={0} | all-to-all | bytes 294912 | tf_op jit(solution)/shard_map/all_to_all | solution.py:313
  35.3 20.1 %all_to_all.16.parts = f32[4,72,256]{2,1,0:T(8,128)S(1)} all-to-all(f32[4,72,256]{2,1,0:T(8,128)S(1)} %shard_map.139), channel_id=1, replica_groups={{0,2,4,6},{1,3,5,7},{8,10,12,14},{9,11,13,15},{16,18,20,22},{17,19,21,2..., dimensions={0} | all-to-all | bytes 589824 | tf_op jit(solution)/shard_map/all_to_all | solution.py:313
  55.4 0.7 %shard_map.140 = (f32[4,4,4,256]{3,2,1,0:T(4,128)}, f32[4,256]{1,0:T(4,128)}, f32[6,6,256]{2,1,0:T(8,128)}, f32[6,256]{1,0:T(8,128)}) custom-call(f32[4,72,256]{2,1,0:T(8,128)S(1)} %all_to_all.16.parts), custom_call_target="tpu_custom_call" | custom-call | flops 1000000 | bytes 200000 | tf_op jit(solution)/shard_map/pallas_call | solution.py:319
  (1 shorter events, 0.0 us)
Async XLA Ops:
  3.3 10.8 %copy-start = (f32[5,1536]{1,0:T(8,128)S(1)}, f32[5,1536]{1,0:T(8,128)}, u32[]{:S(2)}) copy-start(f32[5,1536]{1,0:T(8,128)} %partials.1) | copy-start | bytes 92164
  3.3 10.8 %copy-start.1 = (f32[1536]{0:T(1024)S(1)}, f32[1536]{0:T(1024)}, u32[]{:S(2)}) copy-start(f32[1536]{0:T(1024)} %resid.1) | copy-start | bytes 18436
  3.3 10.8 %copy-start.2 = (f32[1536]{0:T(1024)S(1)}, f32[1536]{0:T(1024)}, u32[]{:S(2)}) copy-start(f32[1536]{0:T(1024)} %weight.1) | copy-start | bytes 18436
  3.3 10.8 %copy-start.3 = (s32[1536]{0:T(1024)S(1)}, s32[1536]{0:T(1024)}, u32[]{:S(2)}) copy-start(s32[1536]{0:T(1024)} %ids.1) | copy-start | bytes 18436
  3.3 22.0 %all-to-all-start = ((f32[64,2,384]{2,1,0:T(2,128)}), f32[64,2,384]{2,1,0:T(2,128)S(1)}, u32[]{:S(2)}, u32[]{:S(2)}) async-start(f32[64,2,384]{2,1,0:T(2,128)} %shard_map.136), calls=%async_computation | async-start | bytes 393216 | tf_op jit(solution)/shard_map/all_to_all | solution.py:364

commit v7 on v6

--- a/solution.py
+++ b/solution.py
@@ -395,7 +395,7 @@
         got,
     )
     pairs = [[2 * g, 2 * g + 1] for g in range(z_count // 2)]
-    ranks = [[2 * g + i for g in range(z_count // 2)] for i in range(2)]
+    ranks = [[2 * g + i for g in reversed(range(z_count // 2))] for i in range(2)]
     parts = exchange(sums, pairs)
     parts = call(middle_kernel, shape(z_count // 2, 72, SEG), [], 8, 1000000, parts)
     parts = exchange(parts, ranks)

time: 56.4 us -> 55.6 us (0.986)
  the two profiles are of different devices: /device:TPU:8 before, /device:TPU:1 now
where the time goes in v7:
time: 55.6 us; the launch traced here: 55.3 us
  blocking collectives  25.5 us (46%)
  starting transfers between devices  11.8 us (21%)
  waiting for transfers between devices  10.2 us (18%)
  Pallas kernels  6.98 us (13%)
  between operations  0.73 us (1%)
    all_to_all x2, blocking collectives, exchange(): lax.all_to_all(blocks, 'src', split_axis=0, concat_axis=0, tiled=True, ax...  25.5 us
    all_to_all x1, starting transfers between devices, local(): got = lax.all_to_all(send, 'tm', split_axis=0, concat_axis=0, tiled=True)  11.8 us
    all_to_all x1, waiting for transfers between devices, local(): got = lax.all_to_all(send, 'tm', split_axis=0, concat_axis=0, tiled=True)  10.2 us
    pallas_call x5, Pallas kernels, call(): pl.pallas_call(kernel, out_shape=out_shape, in_specs=[pl.BlockSpec(memory...  6.98 us
  transfers between devices with their start and end apart: 1, of which 1 were waited for; matrix products, arithmetic and copies ran while one was open for 0% of the time, Pallas kernels for 3%

profile of v7, /device:TPU:1, one launch (start us, length us, event | category | flops | bytes accessed | tf_op | source)
XLA Modules:
  0.0 55.3 jit_solution(1931523846685207319)
XLA Ops:
  0.6 2.6 %shard_map.136 = f32[64,2,384]{2,1,0:T(2,128)} custom-call(f32[4,1536]{1,0:T(4,128)} %refs_0_.1, f32[1536]{0:T(1024)} %refs_1_.1, f32[6,1536]{1,0:T(8,128)} %refs_2_.1, f32[1536]{0:T(1024)} %resid.1, f32[1536]{0:T(1024)} %weight.1, s32[1536]{0:T(1024)} %refs_5_.1, s32[1536]{0:T(1024)} %refs_6_.1), custom_call_target="tpu_custom_call" | custom-call | flops 1000000000 | bytes 200000 | tf_op jit(solution)/shard_map/pallas_call | solution.py:319
  3.3 0.0 copy-start
  3.3 0.0 copy-start.1
  3.3 0.0 copy-start.2
  3.3 0.0 copy-start.3
  3.3 11.8 %all-to-all-start = ((f32[64,2,384]{2,1,0:T(2,128)}), f32[64,2,384]{2,1,0:T(2,128)S(1)}, u32[]{:S(2)}, u32[]{:S(2)}) async-start(f32[64,2,384]{2,1,0:T(2,128)} %shard_map.136), calls=%async_computation | async-start | bytes 393216 | tf_op jit(solution)/shard_map/all_to_all | solution.py:364
  15.1 0.0 copy-done
  15.1 0.0 copy-done.1
  15.1 0.0 copy-done.2
  15.1 0.0 copy-done.3
  15.1 1.8 %shard_map.137 = (f32[5,5,1024]{2,1,0:T(8,128)}, f32[5,1024]{1,0:T(8,128)}) custom-call(f32[5,1536]{1,0:T(8,128)S(1)} %copy-done, f32[1536]{0:T(1024)S(1)} %copy-done.1, f32[1536]{0:T(1024)S(1)} %copy-done.2, s32[1536]{0:T(1024)S(1)} %copy-done.3), custom_call_target="tpu_custom_call" | custom-call | flops 4000000000 | bytes 200000 | tf_op jit(solution)/shard_map/pallas_call | solution.py:319
  16.9 10.2 %all-to-all-done.got = f32[64,2,384]{2,1,0:T(2,128)S(1)} async-done(((f32[64,2,384]{2,1,0:T(2,128)}), f32[64,2,384]{2,1,0:T(2,128)S(1)}, u32[]{:S(2)}, u32[]{:S(2)}) %all-to-all-start) | async-done | bytes 196640 | tf_op jit(solution)/shard_map/all_to_all | solution.py:364
  27.1 1.9 %shard_map.138 = f32[2,72,256]{2,1,0:T(8,128)S(1)} custom-call(f32[64,2,384]{2,1,0:T(2,128)S(1)} %all-to-all-done.got), custom_call_target="tpu_custom_call" | custom-call | flops 1000000000 | bytes 200000 | tf_op jit(solution)/shard_map/pallas_call | solution.py:319
  29.0 6.6 %all_to_all.15.parts = f32[2,72,256]{2,1,0:T(8,128)S(1)} all-to-all(f32[2,72,256]{2,1,0:T(8,128)S(1)} %shard_map.138), channel_id=1, replica_groups={{0,1},{2,3},{4,5},{6,7},{8,9},{10,11},{12,13},{14,15},{16,17},{18,19},{..., dimensions={0} | all-to-all | bytes 294912 | tf_op jit(solution)/shard_map/all_to_all | solution.py:313
  35.6 19.0 %all_to_all.16.parts = f32[4,72,256]{2,1,0:T(8,128)S(1)} all-to-all(f32[4,72,256]{2,1,0:T(8,128)S(1)} %shard_map.139), channel_id=1, replica_groups={{6,4,2,0},{7,5,3,1},{14,12,10,8},{15,13,11,9},{22,20,18,16},{23,21,19,1..., dimensions={0} | all-to-all | bytes 589824 | tf_op jit(solution)/shard_map/all_to_all | solution.py:313
  54.5 0.7 %shard_map.140 = (f32[4,4,4,256]{3,2,1,0:T(4,128)}, f32[4,256]{1,0:T(4,128)}, f32[6,6,256]{2,1,0:T(8,128)}, f32[6,256]{1,0:T(8,128)}) custom-call(f32[4,72,256]{2,1,0:T(8,128)S(1)} %all_to_all.16.parts), custom_call_target="tpu_custom_call" | custom-call | flops 1000000 | bytes 200000 | tf_op jit(solution)/shard_map/pallas_call | solution.py:319
  (1 shorter events, 0.0 us)
Async XLA Ops:
  3.3 11.8 %copy-start = (f32[5,1536]{1,0:T(8,128)S(1)}, f32[5,1536]{1,0:T(8,128)}, u32[]{:S(2)}) copy-start(f32[5,1536]{1,0:T(8,128)} %partials.1) | copy-start | bytes 92164
  3.3 11.8 %copy-start.1 = (f32[1536]{0:T(1024)S(1)}, f32[1536]{0:T(1024)}, u32[]{:S(2)}) copy-start(f32[1536]{0:T(1024)} %resid.1) | copy-start | bytes 18436
  3.3 11.8 %copy-start.2 = (f32[1536]{0:T(1024)S(1)}, f32[1536]{0:T(1024)}, u32[]{:S(2)}) copy-start(f32[1536]{0:T(1024)} %weight.1) | copy-start | bytes 18436
  3.3 11.8 %copy-start.3 = (s32[1536]{0:T(1024)S(1)}, s32[1536]{0:T(1024)}, u32[]{:S(2)}) copy-start(s32[1536]{0:T(1024)} %ids.1) | copy-start | bytes 18436
  3.3 23.8 %all-to-all-start = ((f32[64,2,384]{2,1,0:T(2,128)}), f32[64,2,384]{2,1,0:T(2,128)S(1)}, u32[]{:S(2)}, u32[]{:S(2)}) async-start(f32[64,2,384]{2,1,0:T(2,128)} %shard_map.136), calls=%async_computation | async-start | bytes 393216 | tf_op jit(solution)/shard_map/all_to_all | solution.py:364

commit v8 on v7

--- a/solution.py
+++ b/solution.py
@@ -394,7 +394,7 @@
         1000000000,
         got,
     )
-    pairs = [[2 * g, 2 * g + 1] for g in range(z_count // 2)]
+    pairs = [[2 * g + 1, 2 * g] for g in range(z_count // 2)]
     ranks = [[2 * g + i for g in reversed(range(z_count // 2))] for i in range(2)]
     parts = exchange(sums, pairs)
     parts = call(middle_kernel, shape(z_count // 2, 72, SEG), [], 8, 1000000, parts)

time: 55.6 us -> 54.9 us (0.987); the launches traced: 55.3 us -> 54 us
  blocking collectives: 25.5 us -> 24.2 us
    all_to_all x2, blocking collectives: 25.5 us -> 24.2 us  [exchange(): lax.all_to_all(blocks, 'src', split_axis=0, concat_axis=0, tiled=True, ax...]
where the time goes in v8:
time: 54.9 us; the launch traced here: 54 us
  blocking collectives  24.2 us (44%)
  starting transfers between devices  11.8 us (21%)
  waiting for transfers between devices  10.2 us (19%)
  Pallas kernels  6.98 us (13%)
  between operations  0.73 us (1%)
    all_to_all x2, blocking collectives, exchange(): lax.all_to_all(blocks, 'src', split_axis=0, concat_axis=0, tiled=True, ax...  24.2 us
    all_to_all x1, starting transfers between devices, local(): got = lax.all_to_all(send, 'tm', split_axis=0, concat_axis=0, tiled=True)  11.8 us
    all_to_all x1, waiting for transfers between devices, local(): got = lax.all_to_all(send, 'tm', split_axis=0, concat_axis=0, tiled=True)  10.2 us
    pallas_call x5, Pallas kernels, call(): pl.pallas_call(kernel, out_shape=out_shape, in_specs=[pl.BlockSpec(memory...  6.98 us
  transfers between devices with their start and end apart: 1, of which 1 were waited for; matrix products, arithmetic and copies ran while one was open for 0% of the time, Pallas kernels for 3%

profile of v8, /device:TPU:1, one launch (start us, length us, event | category | flops | bytes accessed | tf_op | source)
XLA Modules:
  0.0 54.0 jit_solution(6204029899210422323)
XLA Ops:
  0.6 2.6 %shard_map.136 = f32[64,2,384]{2,1,0:T(2,128)} custom-call(f32[4,1536]{1,0:T(4,128)} %refs_0_.1, f32[1536]{0:T(1024)} %refs_1_.1, f32[6,1536]{1,0:T(8,128)} %refs_2_.1, f32[1536]{0:T(1024)} %resid.1, f32[1536]{0:T(1024)} %weight.1, s32[1536]{0:T(1024)} %refs_5_.1, s32[1536]{0:T(1024)} %refs_6_.1), custom_call_target="tpu_custom_call" | custom-call | flops 1000000000 | bytes 200000 | tf_op jit(solution)/shard_map/pallas_call | solution.py:319
  3.3 0.0 copy-start
  3.3 0.0 copy-start.1
  3.3 0.0 copy-start.2
  3.3 0.0 copy-start.3
  3.3 11.8 %all-to-all-start = ((f32[64,2,384]{2,1,0:T(2,128)}), f32[64,2,384]{2,1,0:T(2,128)S(1)}, u32[]{:S(2)}, u32[]{:S(2)}) async-start(f32[64,2,384]{2,1,0:T(2,128)} %shard_map.136), calls=%async_computation | async-start | bytes 393216 | tf_op jit(solution)/shard_map/all_to_all | solution.py:364
  15.1 0.0 copy-done
  15.1 0.0 copy-done.1
  15.1 0.0 copy-done.2
  15.1 0.0 copy-done.3
  15.1 1.8 %shard_map.137 = (f32[5,5,1024]{2,1,0:T(8,128)}, f32[5,1024]{1,0:T(8,128)}) custom-call(f32[5,1536]{1,0:T(8,128)S(1)} %copy-done, f32[1536]{0:T(1024)S(1)} %copy-done.1, f32[1536]{0:T(1024)S(1)} %copy-done.2, s32[1536]{0:T(1024)S(1)} %copy-done.3), custom_call_target="tpu_custom_call" | custom-call | flops 4000000000 | bytes 200000 | tf_op jit(solution)/shard_map/pallas_call | solution.py:319
  16.9 10.2 %all-to-all-done.got = f32[64,2,384]{2,1,0:T(2,128)S(1)} async-done(((f32[64,2,384]{2,1,0:T(2,128)}), f32[64,2,384]{2,1,0:T(2,128)S(1)}, u32[]{:S(2)}, u32[]{:S(2)}) %all-to-all-start) | async-done | bytes 196640 | tf_op jit(solution)/shard_map/all_to_all | solution.py:364
  27.1 1.9 %shard_map.138 = f32[2,72,256]{2,1,0:T(8,128)S(1)} custom-call(f32[64,2,384]{2,1,0:T(2,128)S(1)} %all-to-all-done.got), custom_call_target="tpu_custom_call" | custom-call | flops 1000000000 | bytes 200000 | tf_op jit(solution)/shard_map/pallas_call | solution.py:319
  29.0 7.0 %all_to_all.15.parts = f32[2,72,256]{2,1,0:T(8,128)S(1)} all-to-all(f32[2,72,256]{2,1,0:T(8,128)S(1)} %shard_map.138), channel_id=1, replica_groups={{1,0},{3,2},{5,4},{7,6},{9,8},{11,10},{13,12},{15,14},{17,16},{19,18},{..., dimensions={0} | all-to-all | bytes 294912 | tf_op jit(solution)/shard_map/all_to_all | solution.py:313
  36.0 17.2 %all_to_all.16.parts = f32[4,72,256]{2,1,0:T(8,128)S(1)} all-to-all(f32[4,72,256]{2,1,0:T(8,128)S(1)} %shard_map.139), channel_id=1, replica_groups={{6,4,2,0},{7,5,3,1},{14,12,10,8},{15,13,11,9},{22,20,18,16},{23,21,19,1..., dimensions={0} | all-to-all | bytes 589824 | tf_op jit(solution)/shard_map/all_to_all | solution.py:313
  53.3 0.7 %shard_map.140 = (f32[4,4,4,256]{3,2,1,0:T(4,128)}, f32[4,256]{1,0:T(4,128)}, f32[6,6,256]{2,1,0:T(8,128)}, f32[6,256]{1,0:T(8,128)}) custom-call(f32[4,72,256]{2,1,0:T(8,128)S(1)} %all_to_all.16.parts), custom_call_target="tpu_custom_call" | custom-call | flops 1000000 | bytes 200000 | tf_op jit(solution)/shard_map/pallas_call | solution.py:319
  (1 shorter events, 0.0 us)
Async XLA Ops:
  3.3 11.8 %copy-start = (f32[5,1536]{1,0:T(8,128)S(1)}, f32[5,1536]{1,0:T(8,128)}, u32[]{:S(2)}) copy-start(f32[5,1536]{1,0:T(8,128)} %partials.1) | copy-start | bytes 92164
  3.3 11.8 %copy-start.1 = (f32[1536]{0:T(1024)S(1)}, f32[1536]{0:T(1024)}, u32[]{:S(2)}) copy-start(f32[1536]{0:T(1024)} %resid.1) | copy-start | bytes 18436
  3.3 11.8 %copy-start.2 = (f32[1536]{0:T(1024)S(1)}, f32[1536]{0:T(1024)}, u32[]{:S(2)}) copy-start(f32[1536]{0:T(1024)} %weight.1) | copy-start | bytes 18436
  3.3 11.8 %copy-start.3 = (s32[1536]{0:T(1024)S(1)}, s32[1536]{0:T(1024)}, u32[]{:S(2)}) copy-start(s32[1536]{0:T(1024)} %ids.1) | copy-start | bytes 18436
  3.3 23.8 %all-to-all-start = ((f32[64,2,384]{2,1,0:T(2,128)}), f32[64,2,384]{2,1,0:T(2,128)S(1)}, u32[]{:S(2)}, u32[]{:S(2)}) async-start(f32[64,2,384]{2,1,0:T(2,128)} %shard_map.136), calls=%async_computation | async-start | bytes 393216 | tf_op jit(solution)/shard_map/all_to_all | solution.py:364
